TPU v7x, 128 devices: a whole 4x4x4 slice. The times are simulated.
128 devices in a mesh: pr: 16 (over z, x), pc: 8 (over y, core).
Axes of the slice: x: 4, y: 4, z: 4, core: 2. Of those that a mesh axis runs over, the one named last changes fastest.
Arguments:
- trailing: float32 [20480, 20480], P('pr', 'pc'), may hold values from -25 to 25, as said below
- v_panels: float32 [6, 32, 20480], P(None, None, ('pr', 'pc')), may hold values from -0.078125 to 0.078125
- t_panels: float32 [6, 32, 32], replicated, may hold values from -0.2 to 0.5, as said below
Outputs:
- updated: float32 [20480, 20480], P('pr', 'pc')
- w_panels: float32 [6, 32, 20480], P(None, None, ('pr', 'pc'))
Inputs may be any that keep to these rules, and one draw needn't show every extreme that they name: trailing is exactly symmetric. `t_panels`: each panel's factor is upper triangular with diagonal entries of 0.25 to 0.5.
All inputs are finite; a program needn't handle non-finite values.
Results may differ from a plain program's by a relative error of at most 0.00013.
Values sent between devices are 32-bit elements; how exact they have to be, the bound alone decides.
A program may use at most 128 MiB of HBM per device.

v0:
```python
import jax
import jax.numpy as jnp
from jax import lax
from jax.sharding import PartitionSpec as P


def broadcast(value, axis, source):
    kept = jnp.where(lax.axis_index(axis) == source, value, 0).astype(value.dtype)
    return lax.psum(kept, axis)


def contract(left_side, right_side, left_dim, right_dim):
    return lax.dot_general(
        left_side,
        right_side,
        (((left_dim,), (right_dim,)), ((), ())),
        precision=lax.Precision.HIGHEST,
        preferred_element_type=jnp.float32,
    )


def fetch_v_columns(v_row, col_rank, ratio):
    pieces = []
    for offset in range(ratio):
        pieces.append(broadcast(v_row, "pr", col_rank * ratio + offset))
    return jnp.concatenate(pieces, axis=1)


def fetch_w_columns(w_row, col_rank, ratio):
    pieces = []
    for offset in range(ratio):
        pieces.append(broadcast(w_row, "pr", col_rank * ratio + offset))
    return jnp.concatenate(pieces, axis=1)


def per_device(trailing, v_panels, t_panels):
    matrix = trailing
    rows_here = matrix.shape[0]
    col_rank = lax.axis_index("pc")
    ratio = lax.axis_size("pr") // lax.axis_size("pc")
    share = rows_here // lax.axis_size("pc")
    w_blocks = []
    for panel in range(v_panels.shape[0]):
        v_row = lax.all_gather(v_panels[panel], "pc", axis=1, tiled=True)
        v_col = fetch_v_columns(v_row, col_rank, ratio)
        factor = t_panels[panel]
        partial_value = contract(v_col, matrix, 1, 1)
        x_row = lax.psum(partial_value, "pc")
        gram_block = lax.psum(contract(v_row, x_row, 1, 1), "pr")
        middle = contract(contract(factor, gram_block, 0, 0), factor, 1, 0)
        w_row = contract(factor, x_row, 0, 0) - 0.5 * contract(middle, v_row, 0, 0)
        w_col = fetch_w_columns(w_row, col_rank, ratio)
        left_side = jnp.concatenate([v_row, w_row], axis=0)
        right_side = jnp.concatenate([w_col, v_col], axis=0)
        matrix = matrix - contract(left_side, right_side, 0, 0)
        w_blocks.append(lax.dynamic_slice_in_dim(w_row, col_rank * share, share, 1))
    return (matrix, jnp.stack(w_blocks))


def solution(mesh):
    return jax.shard_map(
        per_device,
        mesh=mesh,
        in_specs=(P("pr", "pc"), P(None, None, ("pr", "pc")), P()),
        out_specs=(P("pr", "pc"), P(None, None, ("pr", "pc"))),
        check_vma=False,
    )
```

profile of v0, /device:TPU:1, one launch (start us, length us, event | category | flops | bytes accessed | tf_op | source)
XLA Modules:
  0.0 1610.0 jit_solution(2257900202977496059)
XLA Ops:
  8.2 15.1 all-gather
  24.6 13.2 all-gather.1
  38.1 70.0 %all-reduce.45.cloned.1.call-done = (f32[32,1280]{1,0:T(8,128)}, f32[32,1280]{1,0:T(8,128)}) async-done(((f32[32,1280]{1,0:T(8,128)}, f32[32,1280]{1,0:T(8,128)}), (f32[32,1280]{1,0:T(8,128)}, f32[32,1280]{1,0:T(8,128)})) %all-reduce.45.cloned.1.call-update) | async-done | bytes 327696 | tf_op jit(solution)/shard_map/psum | solution.py:9
  110.0 15.3 fusion.109
  126.2 57.3 %all-reduce.21.cloned.1.call-done = f32[32,1280]{1,0:T(8,128)} async-done(((f32[32,1280]{1,0:T(8,128)}), f32[32,1280]{1,0:T(8,128)}) %all-reduce.21.cloned.1.call-update) | async-done | bytes 163856 | tf_op jit(solution)/shard_map/psum | solution.py:48
  183.5 1.4 convolution_bitcast_fusion.11
  184.9 60.8 %psum.255 = f32[32,32]{0,1:T(8,128)S(1)} all-reduce(f32[32,32]{0,1:T(8,128)S(1)} %convolution_bitcast_fusion.11), channel_id=1, replica_groups=mesh['pr'=16,'pc'=8] {'pr'}, use_global_device_ids=true, to_apply=%region_3.4 | all-reduce | flops 1024 | bytes 8192 | tf_op jit(solution)/shard_map/psum | solution.py:49
  246.0 1.3 convolution_bitcast_fusion.5
  247.3 1.5 broadcast_select_fusion.21
  248.9 28.3 %all-gather.2 = f32[1,32,1280]{1,0,2:T(1,128)S(1)} all-gather(f32[1,32,160]{1,0,2:T(1,128)S(1)} %copy.19), channel_id=4, replica_groups=mesh['pr'=16,'pc'=8] {'pc'}, dimensions={2}, use_global_device_ids=true | all-gather | bytes 184320 | tf_op jit(solution)/shard_map/all_gather | solution.py:44
  277.6 63.6 %all-reduce.43.cloned.1.call-done = (f32[32,1280]{1,0:T(8,128)}, f32[32,1280]{1,0:T(8,128)}, f32[32,1280]{1,0:T(8,128)}, f32[32,1280]{1,0:T(8,128)}) async-done(((f32[32,1280]{1,0:T(8,128)}, f32[32,1280]{1,0:T(8,128)}, f32[32,1280]{1,0:T(8,128)}, f32[32,1280]{1,0:T(8,128)}), (f32[32,1280]{1,0:T(8,128)}, f32[32,1280]{1,0:T(8,128)}, f32[32,1280]{1,0:T(8,128)}, ...) | async-done | bytes 655376 | tf_op jit(solution)/shard_map/psum | solution.py:9
  342.1 0.9 constant_dynamic-update-slice_fusion.2
  343.1 14.6 convolution_subtract_fusion.5
  357.7 4.9 copy-done.3
  362.6 12.4 fusion.110
  375.9 57.3 %all-reduce.23.cloned.1.call-done = f32[32,1280]{1,0:T(8,128)} async-done(((f32[32,1280]{1,0:T(8,128)}), f32[32,1280]{1,0:T(8,128)}) %all-reduce.23.cloned.1.call-update) | async-done | bytes 163856 | tf_op jit(solution)/shard_map/psum | solution.py:48
  433.2 1.4 convolution_bitcast_fusion.10
  434.6 60.8 %psum.261 = f32[32,32]{0,1:T(8,128)S(1)} all-reduce(f32[32,32]{0,1:T(8,128)S(1)} %convolution_bitcast_fusion.10), channel_id=1, replica_groups=mesh['pr'=16,'pc'=8] {'pr'}, use_global_device_ids=true, to_apply=%region_9.10 | all-reduce | flops 1024 | bytes 8192 | tf_op jit(solution)/shard_map/psum | solution.py:49
  495.7 1.3 convolution_bitcast_fusion.4
  497.0 1.5 broadcast_select_fusion.17
  498.7 28.1 %all-gather.3 = f32[1,32,1280]{1,0,2:T(1,128)S(1)} all-gather(f32[1,32,160]{1,0,2:T(1,128)S(1)} %copy.20), channel_id=5, replica_groups=mesh['pr'=16,'pc'=8] {'pc'}, dimensions={2}, use_global_device_ids=true | all-gather | bytes 184320 | tf_op jit(solution)/shard_map/all_gather | solution.py:44
  526.7 12.1 copy.12
  538.9 52.2 %all-reduce.41.cloned.1.call-done = (f32[32,1280]{1,0:T(8,128)}, f32[32,1280]{1,0:T(8,128)}, f32[32,1280]{1,0:T(8,128)}, f32[32,1280]{1,0:T(8,128)}) async-done(((f32[32,1280]{1,0:T(8,128)}, f32[32,1280]{1,0:T(8,128)}, f32[32,1280]{1,0:T(8,128)}, f32[32,1280]{1,0:T(8,128)}), (f32[32,1280]{1,0:T(8,128)}, f32[32,1280]{1,0:T(8,128)}, f32[32,1280]{1,0:T(8,128)}, ...) | async-done | bytes 655376 | tf_op jit(solution)/shard_map/psum | solution.py:9
  592.9 14.2 convolution_subtract_fusion.4
  607.2 4.9 copy-done.2
  612.1 12.4 fusion.111
  625.4 57.4 %all-reduce.25.cloned.1.call-done = f32[32,1280]{1,0:T(8,128)} async-done(((f32[32,1280]{1,0:T(8,128)}), f32[32,1280]{1,0:T(8,128)}) %all-reduce.25.cloned.1.call-update) | async-done | bytes 163856 | tf_op jit(solution)/shard_map/psum | solution.py:48
  682.7 1.4 convolution_bitcast_fusion.9
  684.1 60.8 %psum.267 = f32[32,32]{0,1:T(8,128)S(1)} all-reduce(f32[32,32]{0,1:T(8,128)S(1)} %convolution_bitcast_fusion.9), channel_id=1, replica_groups=mesh['pr'=16,'pc'=8] {'pr'}, use_global_device_ids=true, to_apply=%region_15.16 | all-reduce | flops 1024 | bytes 8192 | tf_op jit(solution)/shard_map/psum | solution.py:49
  745.2 1.3 convolution_bitcast_fusion.3
  746.5 1.5 broadcast_select_fusion.13
  748.2 28.1 %all-gather.4 = f32[1,32,1280]{1,0,2:T(1,128)S(1)} all-gather(f32[1,32,160]{1,0,2:T(1,128)S(1)} %copy.21), channel_id=6, replica_groups=mesh['pr'=16,'pc'=8] {'pc'}, dimensions={2}, use_global_device_ids=true | all-gather | bytes 184320 | tf_op jit(solution)/shard_map/all_gather | solution.py:44
  777.0 63.5 %all-reduce.39.cloned.1.call-done = (f32[32,1280]{1,0:T(8,128)}, f32[32,1280]{1,0:T(8,128)}, f32[32,1280]{1,0:T(8,128)}, f32[32,1280]{1,0:T(8,128)}) async-done(((f32[32,1280]{1,0:T(8,128)}, f32[32,1280]{1,0:T(8,128)}, f32[32,1280]{1,0:T(8,128)}, f32[32,1280]{1,0:T(8,128)}), (f32[32,1280]{1,0:T(8,128)}, f32[32,1280]{1,0:T(8,128)}, f32[32,1280]{1,0:T(8,128)}, ...) | async-done | bytes 655376 | tf_op jit(solution)/shard_map/psum | solution.py:9
  842.4 14.2 convolution_subtract_fusion.3
  856.6 4.9 copy-done.1
  861.6 12.4 fusion.112
  874.8 57.3 %all-reduce.27.cloned.1.call-done = f32[32,1280]{1,0:T(8,128)} async-done(((f32[32,1280]{1,0:T(8,128)}), f32[32,1280]{1,0:T(8,128)}) %all-reduce.27.cloned.1.call-update) | async-done | bytes 163856 | tf_op jit(solution)/shard_map/psum | solution.py:48
  932.2 1.4 convolution_bitcast_fusion.8
  933.6 60.8 %psum.273 = f32[32,32]{0,1:T(8,128)S(1)} all-reduce(f32[32,32]{0,1:T(8,128)S(1)} %convolution_bitcast_fusion.8), channel_id=1, replica_groups=mesh['pr'=16,'pc'=8] {'pr'}, use_global_device_ids=true, to_apply=%region_21.22 | all-reduce | flops 1024 | bytes 8192 | tf_op jit(solution)/shard_map/psum | solution.py:49
  994.7 1.3 convolution_bitcast_fusion.2
  996.0 1.5 broadcast_select_fusion.9
  997.6 28.1 %all-gather.5 = f32[1,32,1280]{1,0,2:T(1,128)S(1)} all-gather(f32[1,32,160]{1,0,2:T(1,128)S(1)} %copy.22), channel_id=7, replica_groups=mesh['pr'=16,'pc'=8] {'pc'}, dimensions={2}, use_global_device_ids=true | all-gather | bytes 184320 | tf_op jit(solution)/shard_map/all_gather | solution.py:44
  1026.2 63.8 %all-reduce.37.cloned.1.call-done = (f32[32,1280]{1,0:T(8,128)}, f32[32,1280]{1,0:T(8,128)}, f32[32,1280]{1,0:T(8,128)}, f32[32,1280]{1,0:T(8,128)}) async-done(((f32[32,1280]{1,0:T(8,128)}, f32[32,1280]{1,0:T(8,128)}, f32[32,1280]{1,0:T(8,128)}, f32[32,1280]{1,0:T(8,128)}), (f32[32,1280]{1,0:T(8,128)}, f32[32,1280]{1,0:T(8,128)}, f32[32,1280]{1,0:T(8,128)}, ...) | async-done | bytes 655376 | tf_op jit(solution)/shard_map/psum | solution.py:9
  1090.9 0.9 constant_dynamic-update-slice_fusion.8
  1091.9 14.2 convolution_subtract_fusion.2
  1106.1 4.9 copy-done
  1111.1 12.4 fusion.113
  1124.3 57.4 %all-reduce.29.cloned.1.call-done = f32[32,1280]{1,0:T(8,128)} async-done(((f32[32,1280]{1,0:T(8,128)}), f32[32,1280]{1,0:T(8,128)}) %all-reduce.29.cloned.1.call-update) | async-done | bytes 163856 | tf_op jit(solution)/shard_map/psum | solution.py:48
  1181.7 1.4 convolution_bitcast_fusion.7
  1183.1 60.8 %psum.279 = f32[32,32]{0,1:T(8,128)S(1)} all-reduce(f32[32,32]{0,1:T(8,128)S(1)} %convolution_bitcast_fusion.7), channel_id=1, replica_groups=mesh['pr'=16,'pc'=8] {'pr'}, use_global_device_ids=true, to_apply=%region_27.28 | all-reduce | flops 1024 | bytes 8192 | tf_op jit(solution)/shard_map/psum | solution.py:49
  1244.2 1.3 convolution_bitcast_fusion.1
  1245.5 1.5 broadcast_select_fusion.5
  1247.2 92.3 %all-reduce.35.cloned.1.call-done = (f32[32,1280]{1,0:T(8,128)}, f32[32,1280]{1,0:T(8,128)}, f32[32,1280]{1,0:T(8,128)}, f32[32,1280]{1,0:T(8,128)}) async-done(((f32[32,1280]{1,0:T(8,128)}, f32[32,1280]{1,0:T(8,128)}, f32[32,1280]{1,0:T(8,128)}, f32[32,1280]{1,0:T(8,128)}), (f32[32,1280]{1,0:T(8,128)}, f32[32,1280]{1,0:T(8,128)}, f32[32,1280]{1,0:T(8,128)}, ...) | async-done | bytes 655376 | tf_op jit(solution)/shard_map/psum | solution.py:9
  1340.4 0.9 constant_dynamic-update-slice_fusion.10
  1341.4 14.5 convolution_subtract_fusion.1
  1355.8 4.9 copy-done.4
  1360.8 12.4 fusion.114
  1373.4 58.0 %all-reduce.31.cloned.1.call-done = f32[32,1280]{1,0:T(8,128)} async-done(((f32[32,1280]{1,0:T(8,128)}), f32[32,1280]{1,0:T(8,128)}) %all-reduce.31.cloned.1.call-update) | async-done | bytes 163856 | tf_op jit(solution)/shard_map/psum | solution.py:48
  1431.4 1.4 convolution_bitcast_fusion.6
  1432.8 61.1 %psum.285 = f32[32,32]{0,1:T(8,128)S(1)} all-reduce(f32[32,32]{0,1:T(8,128)S(1)} %convolution_bitcast_fusion.6), channel_id=1, replica_groups=mesh['pr'=16,'pc'=8] {'pr'}, use_global_device_ids=true, to_apply=%region_33.34 | all-reduce | flops 1024 | bytes 8192 | tf_op jit(solution)/shard_map/psum | solution.py:49
  1494.2 1.3 convolution_bitcast_fusion
  1495.5 1.5 broadcast_select_fusion.1
  1497.3 90.3 %all-reduce.33.cloned.1.call-done = (f32[32,1280]{1,0:T(8,128)}, f32[32,1280]{1,0:T(8,128)}) async-done(((f32[32,1280]{1,0:T(8,128)}, f32[32,1280]{1,0:T(8,128)}), (f32[32,1280]{1,0:T(8,128)}, f32[32,1280]{1,0:T(8,128)})) %all-reduce.33.cloned.1.call-update) | async-done | bytes 327696 | tf_op jit(solution)/shard_map/psum | solution.py:9
  1587.5 15.4 convolution_subtract_fusion
  (80 shorter events, 19.9 us)
Async XLA Ops:
  7.2 238.5 %copy-start.5 = (f32[6,32,32]{2,1,0:T(8,128)S(1)}, f32[6,32,32]{2,1,0:T(8,128)}, u32[]{:S(2)}) copy-start(f32[6,32,32]{2,1,0:T(8,128)} %param.5) | copy-start | bytes 73732
  7.2 101.0 %all-reduce.45.cloned.1.call-start = ((), (), s32[]{:S(2)}) async-start(), calls=%async_computation.12 | async-start | bytes 655360 | tf_op jit(solution)/shard_map/psum | solution.py:9
  24.4 159.1 %all-reduce.21.cloned.1.call-start = ((), (), s32[]{:S(2)}) async-start(), calls=%async_computation | async-start | bytes 327680 | tf_op jit(solution)/shard_map/psum | solution.py:48
  125.4 215.8 %all-reduce.43.cloned.1.call-start = ((), (), s32[]{:S(2)}) async-start(), calls=%async_computation.11 | async-start | bytes 1310720 | tf_op jit(solution)/shard_map/psum | solution.py:9
  248.8 184.4 %all-reduce.23.cloned.1.call-start = ((), (), s32[]{:S(2)}) async-start(), calls=%async_computation.1 | async-start | bytes 327680 | tf_op jit(solution)/shard_map/psum | solution.py:48
  357.6 5.0 copy-start.3
  375.1 216.0 %all-reduce.41.cloned.1.call-start = ((), (), s32[]{:S(2)}) async-start(), calls=%async_computation.10 | async-start | bytes 1310720 | tf_op jit(solution)/shard_map/psum | solution.py:9
  498.5 184.2 %all-reduce.25.cloned.1.call-start = ((), (), s32[]{:S(2)}) async-start(), calls=%async_computation.2 | async-start | bytes 327680 | tf_op jit(solution)/shard_map/psum | solution.py:48
  607.1 5.0 copy-start.2
  624.6 215.9 %all-reduce.39.cloned.1.call-start = ((), (), s32[]{:S(2)}) async-start(), calls=%async_computation.9 | async-start | bytes 1310720 | tf_op jit(solution)/shard_map/psum | solution.py:9
  748.0 184.1 %all-reduce.27.cloned.1.call-start = ((), (), s32[]{:S(2)}) async-start(), calls=%async_computation.3 | async-start | bytes 327680 | tf_op jit(solution)/shard_map/psum | solution.py:48
  856.6 5.0 copy-start.1
  874.0 216.0 %all-reduce.37.cloned.1.call-start = ((), (), s32[]{:S(2)}) async-start(), calls=%async_computation.8 | async-start | bytes 1310720 | tf_op jit(solution)/shard_map/psum | solution.py:9
  997.5 184.2 %all-reduce.29.cloned.1.call-start = ((), (), s32[]{:S(2)}) async-start(), calls=%async_computation.4 | async-start | bytes 327680 | tf_op jit(solution)/shard_map/psum | solution.py:48
  1106.1 5.0 copy-start
  1123.5 215.9 %all-reduce.35.cloned.1.call-start = ((), (), s32[]{:S(2)}) async-start(), calls=%async_computation.7 | async-start | bytes 1310720 | tf_op jit(solution)/shard_map/psum | solution.py:9
  1247.0 184.4 %all-reduce.31.cloned.1.call-start = ((), (), s32[]{:S(2)}) async-start(), calls=%async_computation.5 | async-start | bytes 327680 | tf_op jit(solution)/shard_map/psum | solution.py:48
  1355.8 5.0 copy-start.4
  1373.2 214.3 %all-reduce.33.cloned.1.call-start = ((), (), s32[]{:S(2)}) async-start(), calls=%async_computation.6 | async-start | bytes 655360 | tf_op jit(solution)/shard_map/psum | solution.py:9
  1497.3 105.7 %copy-start.6 = (f32[6,32,160]{2,1,0:T(8,128)}, f32[6,32,160]{2,1,0:T(8,128)S(1)}, u32[]{:S(2)}) copy-start(f32[6,32,160]{2,1,0:T(8,128)S(1)} %constant_dynamic-update-slice_fusion.12) | copy-start | bytes 368644
Sparse Core Ops, SparseCore 0:
  24.5 83.5 all-reduce.44
  125.5 57.9 all-reduce.20
  248.9 92.2 all-reduce.42
  375.2 57.9 all-reduce.22
  498.6 92.3 all-reduce.40
  624.7 57.9 all-reduce.24
  748.2 92.3 all-reduce.38
  874.2 57.9 all-reduce.26
  997.6 92.3 all-reduce.36
  1123.7 57.9 all-reduce.28
  1247.1 92.3 all-reduce.34
  1373.4 57.9 all-reduce.30
  1497.2 90.3 all-reduce.32
where the time goes:
time: 1620 us; the launch traced here: 1610 us
  waiting for transfers between devices  841 us (52%)
  blocking collectives  506 us (31%)
  matrix products  192 us (12%)
  local copies, waits for them, and re-layouts  52.1 us (3%)
    psum x7, waiting for transfers between devices, broadcast(): return lax.psum(kept, axis)  496 us
    psum x6, blocking collectives, per_device(): gram_block = lax.psum(contract(v_row, x_row, 1, 1), 'pr')  365 us
    psum x6, waiting for transfers between devices, per_device(): x_row = lax.psum(partial_value, 'pc')  345 us
    dot_general x42, matrix products, contract(): lax.dot_general(left_side, right_side, (((left_dim,), (right_dim,)), ((),...  192 us
    all_gather x6, blocking collectives, per_device(): v_row = lax.all_gather(v_panels[panel], 'pc', axis=1, tiled=True)  141 us
  transfers between devices with their start and end apart: 13, of which 13 were waited for; matrix products, arithmetic and copies ran while one was open for 1% of the time, Pallas kernels for 0%

commit v1 on v0

v1 whole, which is shorter than its diff:
```python
import jax
import jax.numpy as jnp
from jax import lax
from jax.sharding import PartitionSpec as P

HIGHEST = lax.Precision.HIGHEST


def contract(left_side, right_side, left_dim, right_dim, precision=HIGHEST):
    return lax.dot_general(
        left_side,
        right_side,
        (((left_dim,), (right_dim,)), ((), ())),
        precision=precision,
        preferred_element_type=jnp.float32,
    )


def small_coefficients(gram_y, gram_v, t_panels):
    panels, width, _ = t_panels.shape
    size = panels * width
    eye = jnp.eye(size, dtype=jnp.float32)
    zero = jnp.zeros((size, size), jnp.float32)
    of_y = jnp.concatenate([gram_y, zero, eye], axis=1)
    of_v = jnp.concatenate([gram_v, eye, zero], axis=1)
    of_w = []
    for panel in range(panels):
        here = slice(panel * width, (panel + 1) * width)
        of_x = of_y[here]
        if panel:
            done = jnp.concatenate(of_w, axis=0)
            before = slice(0, panel * width)
            left = jnp.concatenate([done[:, here], gram_v[before, here]], axis=0)
            right = jnp.concatenate([of_v[before], done], axis=0)
            of_x = of_x - contract(left, right, 0, 0)
        factor = t_panels[panel]
        scaled = contract(factor, of_x, 0, 0)
        middle = contract(scaled[:, here], factor, 1, 0)
        of_w.append(scaled - 0.5 * contract(middle, of_v[here], 1, 0))
    return jnp.concatenate(of_w, axis=0)


def per_device(trailing, v_panels, t_panels):
    rows, cols = lax.axis_size("pr"), lax.axis_size("pc")
    ratio = rows // cols
    panels, width, share = v_panels.shape
    size = panels * width
    v_own = v_panels.reshape(size, share)
    moves = []
    for i in range(rows):
        for j in range(cols):
            moves.append((i * cols + j, ((i % ratio) * cols + j) * cols + i // ratio))

    def columns(own):
        return lax.all_gather(lax.ppermute(own, ("pr", "pc"), moves), "pr", axis=1, tiled=True)

    v_row = lax.all_gather(v_own, "pc", axis=1, tiled=True)
    v_col = columns(v_own)
    partial_y = contract(v_col, trailing, 1, 1, lax.Precision.HIGH)
    y_own = lax.psum_scatter(partial_y, "pc", scatter_dimension=1, tiled=True)
    y_row = lax.all_gather(y_own, "pc", axis=1, tiled=True)
    y_col = columns(y_own)
    grams = contract(v_own, jnp.concatenate([y_own, v_own], axis=0), 1, 1)
    grams = lax.psum(grams, ("pr", "pc"))
    coefs = small_coefficients(grams[:, :size], grams[:, size:], t_panels)
    of_v, of_y = coefs[:, size : 2 * size], coefs[:, 2 * size :]
    w_own = contract(of_v, v_own, 1, 0) + contract(of_y, y_own, 1, 0)
    left_v = contract(of_v + of_v.T, v_row, 1, 0) + contract(of_y, y_row, 1, 0)
    left_y = contract(of_y, v_row, 0, 0)
    left = jnp.concatenate([left_v, left_y], axis=0)
    right = jnp.concatenate([v_col, y_col], axis=0)
    matrix = trailing - contract(left, right, 0, 0, lax.Precision.HIGH)
    return (matrix, w_own.reshape(panels, width, share))


def solution(mesh):
    return jax.shard_map(
        per_device,
        mesh=mesh,
        in_specs=(P("pr", "pc"), P(None, None, ("pr", "pc")), P()),
        out_specs=(P("pr", "pc"), P(None, None, ("pr", "pc"))),
        check_vma=False,
    )
```

time: 1620 us -> 355 us (0.22)
  waiting for transfers between devices: 841 us -> 190 us
  blocking collectives: 506 us -> 36.6 us
  matrix products: 192 us -> 74.1 us
  local copies, waits for them, and re-layouts: 52.1 us -> 24.1 us
    psum x13 -> x1, waiting for transfers between devices: 840 us -> 118 us  [per_device(): grams = lax.psum(grams, ('pr', 'pc'))]
    psum x6 -> x0, blocking collectives: 365 us -> none  [per_device(): gram_block = lax.psum(contract(v_row, x_row, 1, 1), 'pr')]
    dot_general x42 -> x31, matrix products: 192 us -> 74.1 us  [contract(): lax.dot_general(left_side, right_side, (((left_dim,), (right_dim,)), ((),...]
    all_gather x6 -> x2, blocking collectives: 141 us -> 36.6 us  [the longest x1 20.7 us: per_device(): y_row = lax.all_gather(y_own, 'pc', axis=1, tiled=True)]
    all_gather x0 -> x2, waiting for transfers between devices: none -> 53.5 us  [columns(): lax.all_gather(lax.ppermute(own, ('pr', 'pc'), moves), 'pr', axis=1, tile...]
    unnamed x31 -> x16, local copies, waits for them, and re-layouts: 31.3 us -> 4.28 us
    slice x1 -> x21, local copies, waits for them, and re-layouts: 0.86 us -> 18 us  [the longest x15 14.3 us: small_coefficients(): left = jnp.concatenate([done[:, here], gram_v[before, here]], axis=0)]
  transfers between devices with their start and end apart: 13 -> 6, of which waited for: 13 -> 4; matrix products, arithmetic and copies ran while one was open for 1% -> 18% of each run, Pallas kernels for 0% -> 0%
where the time goes in v1:
time: 355 us; the launch traced here: 354 us
  waiting for transfers between devices  190 us (54%)
  matrix products  74.1 us (21%)
  blocking collectives  36.6 us (10%)
  local copies, waits for them, and re-layouts  24.1 us (7%)
  between operations  14 us (4%)
  starting transfers between devices  11 us (3%)
  other arithmetic  4.12 us (1%)
    psum x1, waiting for transfers between devices, per_device(): grams = lax.psum(grams, ('pr', 'pc'))  118 us
    dot_general x31, matrix products, contract(): lax.dot_general(left_side, right_side, (((left_dim,), (right_dim,)), ((),...  74.1 us
    all_gather x2, waiting for transfers between devices, columns(): lax.all_gather(lax.ppermute(own, ('pr', 'pc'), moves), 'pr', axis=1, tile...  53.5 us
    all_gather x1, blocking collectives, per_device(): y_row = lax.all_gather(y_own, 'pc', axis=1, tiled=True)  20.7 us
    all_gather x1, blocking collectives, per_device(): v_row = lax.all_gather(v_own, 'pc', axis=1, tiled=True)  15.8 us
    slice x15, local copies, waits for them, and re-layouts, small_coefficients(): left = jnp.concatenate([done[:, here], gram_v[before, here]], axis=0)  14.3 us
    reduce_scatter x1, waiting for transfers between devices, per_device(): y_own = lax.psum_scatter(partial_y, 'pc', scatter_dimension=1, tiled=True)  13.6 us
    ppermute x2, starting transfers between devices, columns(): lax.ppermute(own, ('pr', 'pc'), moves)  10.8 us
  transfers between devices with their start and end apart: 6, of which 4 were waited for; matrix products, arithmetic and copies ran while one was open for 18% of the time, Pallas kernels for 0%

profile of v1, /device:TPU:1, one launch (start us, length us, event | category | flops | bytes accessed | tf_op | source)
XLA Modules:
  0.0 353.8 jit_solution(15385846826090534265)
XLA Ops:
  7.2 1.0 copy.12
  8.2 4.5 %collective-permute-start = (f32[192,160]{0,1:T(8,128)S(1)}, f32[192,160]{0,1:T(8,128)S(1)}, u32[]{:S(2)}, u32[]{:S(2)}) collective-permute-start(f32[192,160]{0,1:T(8,128)S(1)} %copy.12), channel_id=1, source_target_pairs={{0,0},{1,8},{2,16},{3,24},{4,32},{5,40},{6,48},{7,56},{8,64},{9,72... | collective-permute-start | bytes 368648 | tf_op jit(solution)/shard_map/ppermute | solution.py:55
  12.8 4.5 %collective-permute-done = f32[192,160]{0,1:T(8,128)S(1)} collective-permute-done((f32[192,160]{0,1:T(8,128)S(1)}, f32[192,160]{0,1:T(8,128)S(1)}, u32[]{:S(2)}, u32[]{:S(2)}) %collective-permute-start) | collective-permute-done | bytes 122912 | tf_op jit(solution)/shard_map/ppermute | solution.py:55
  18.0 53.5 %all-gather.3.cloned.1.call-done = f32[192,2560]{0,1:T(8,128)} async-done(((f32[192,160]{0,1:T(8,128)}), f32[192,2560]{0,1:T(8,128)}) %all-gather.3.cloned.1.call-update) | async-done | bytes 1966096 | tf_op jit(solution)/shard_map/all_gather | solution.py:55
  71.5 9.9 %fusion.106 = f32[192,1280]{0,1:T(8,128)} fusion(f32[192,2560]{0,1:T(8,128)} %all-gather.3.cloned.1.call-done, f32[1280,2560]{1,0:T(8,128)} %param.3), kind=kOutput, calls=%fused_computation.158 | convolution fusion | flops 3774873600 | bytes 16056320 | tf_op jit(solution)/shard_map/dot_general | solution.py:10
  81.5 0.7 fusion.29
  82.2 15.8 %all_gather.13 = f32[192,1280]{0,1:T(8,128)S(1)} all-gather(f32[192,160]{0,1:T(8,128)S(1)} %copy.12), channel_id=1, replica_groups=mesh['pr'=16,'pc'=8] {'pc'}, dimensions={1}, use_global_device_ids=true | all-gather | bytes 1105920 | tf_op jit(solution)/shard_map/all_gather | solution.py:57
  98.0 13.6 %reduce-scatter.2.cloned.1.call-done = f32[192,160]{0,1:T(8,128)} async-done(((f32[192,1280]{0,1:T(8,128)}), f32[192,160]{0,1:T(8,128)}) %reduce-scatter.2.cloned.1.call-update) | async-done | bytes 122896 | tf_op jit(solution)/shard_map/reduce_scatter | solution.py:60
  111.6 2.2 convolution_bitcast_fusion
  113.9 6.3 %collective-permute-start.1 = (f32[192,160]{0,1:T(8,128)}, f32[192,160]{0,1:T(8,128)S(1)}, u32[]{:S(2)}, u32[]{:S(2)}) collective-permute-start(f32[192,160]{0,1:T(8,128)} %reduce-scatter.2.cloned.1.call-done), channel_id=1, source_target_pairs={{0,0},{1,8},{2,16},{3,24},{4,32},{5,40},{6,48},{7,56},{8,64},{9,72... | collective-permute-start | bytes 368648 | tf_op jit(solution)/shard_map/ppermute | solution.py:55
  120.2 20.7 %all_gather.14 = f32[192,1280]{0,1:T(8,128)S(1)} all-gather(f32[192,160]{0,1:T(8,128)} %reduce-scatter.2.cloned.1.call-done), channel_id=1, replica_groups=mesh['pr'=16,'pc'=8] {'pc'}, dimensions={1}, use_global_device_ids=true | all-gather | bytes 1105920 | tf_op jit(solution)/shard_map/all_gather | solution.py:61
  140.9 0.7 copy-done.4
  141.6 118.4 %all-reduce.2.cloned.1.call-done = f32[192,384]{1,0:T(8,128)} async-done(((f32[192,384]{1,0:T(8,128)}), f32[192,384]{1,0:T(8,128)}) %all-reduce.2.cloned.1.call-update) | async-done | bytes 294928 | tf_op jit(solution)/shard_map/psum | solution.py:64
  260.0 1.1 fusion.105
  261.2 2.0 pad_maximum_fusion.1
  263.2 0.7 slice.186
  263.9 0.7 slice.191
  264.6 0.8 slice_dynamic-update-slice_fusion.1
  265.4 0.8 slice_dynamic-update-slice_fusion
  266.1 0.8 slice.185
  267.6 0.9 slice.190
  268.5 0.7 copy.17
  269.1 1.2 convolution_bitcast_fusion.6
  270.3 0.9 fusion.66
  271.2 0.9 constant_dynamic-update-slice_fusion.8
  272.2 0.8 slice.181
  272.9 1.2 convolution_subtract_fusion.3
  274.1 1.0 convolution_bitcast_fusion.5
  275.1 0.9 fusion.64
  276.0 0.9 constant_dynamic-update-slice_fusion.7
  277.0 0.8 copy-done.6
  277.9 1.3 convolution_subtract_fusion.5
  279.2 1.0 convolution_bitcast_fusion.4
  280.2 0.9 fusion.62
  281.1 1.0 constant_dynamic-update-slice_fusion.6
  282.1 0.7 pad_maximum_fusion.5
  282.8 1.5 copy.16
  284.2 1.5 convolution_subtract_fusion.4
  285.8 1.0 convolution_bitcast_fusion.3
  287.4 1.5 fusion.60
  288.9 1.5 slice.195
  290.5 1.5 copy.19
  292.0 1.6 slice.201
  293.6 1.6 copy.21
  295.2 1.9 constant_dynamic-update-slice_fusion.5
  297.7 0.9 copy.18
  298.6 1.6 convolution_subtract_fusion.2
  300.2 1.0 convolution_bitcast_fusion.2
  301.2 0.9 fusion.58
  302.0 0.9 constant_dynamic-update-slice_fusion.4
  303.0 1.0 slice.200
  303.9 0.7 copy.20
  304.6 1.8 convolution_subtract_fusion.1
  306.4 1.0 convolution_bitcast_fusion.1
  307.4 0.9 fusion.56
  308.3 0.9 fusion.7
  309.2 1.1 slice.205
  310.3 1.3 fusion.30
  311.5 1.6 convolution_add_fusion.1
  313.1 0.8 copy.24
  314.0 3.9 %fusion.32 = f32[192,1280]{1,0:T(8,128)} fusion(f32[192,1280]{0,1:T(8,128)S(1)} %all_gather.13, f32[192,576]{1,0:T(8,128)} %fusion.7), kind=kOutput, calls=%fused_computation.59 | convolution fusion | flops 566231040 | bytes 2162688 | tf_op jit(solution)/shard_map/dot_general | solution.py:10
  317.9 2.4 fusion.28
  320.4 3.4 convolution_add_fusion
  323.8 23.5 %convolution_subtract_fusion = f32[1280,2560]{1,0:T(8,128)} fusion(f32[1280,2560]{1,0:T(8,128)} %param.3, f32[192,2560]{0,1:T(8,128)} %all-gather.5.cloned.1.call-done, f32[192,2560]{0,1:T(8,128)} %all-gather.3.cloned.1.call-done, f32[192,1280]{1,0:T(8,128)S(1)} %copy-done, f32[192,1280]{1,0:T(8,128)} %convolution_add_fusion), kind=kOutput, calls=%fused_computation | convolution fusion | flops 7554498560 | bytes 32112640 | tf_op jit(solution)/shard_map/dot_general | solution.py:10
  (30 shorter events, 3.2 us)
Async XLA Ops:
  7.2 64.3 %all-gather.3.cloned.1.call-start = ((), (), s32[]{:S(2)}) async-start(), calls=%async_computation.1 | async-start | bytes 2785280 | tf_op jit(solution)/shard_map/all_gather | solution.py:55
  8.2 9.0 %collective-permute-start = (f32[192,160]{0,1:T(8,128)S(1)}, f32[192,160]{0,1:T(8,128)S(1)}, u32[]{:S(2)}, u32[]{:S(2)}) collective-permute-start(f32[192,160]{0,1:T(8,128)S(1)} %copy.12), channel_id=1, source_target_pairs={{0,0},{1,8},{2,16},{3,24},{4,32},{5,40},{6,48},{7,56},{8,64},{9,72... | collective-permute-start | bytes 368648 | tf_op jit(solution)/shard_map/ppermute | solution.py:55
  17.3 0.7 copy-start.5
  18.0 93.6 %reduce-scatter.2.cloned.1.call-start = ((), (), s32[]{:S(2)}) async-start(), calls=%async_computation.2 | async-start | bytes 1474560 | tf_op jit(solution)/shard_map/reduce_scatter | solution.py:60
  81.4 30.2 %copy-start.1 = (f32[6,32,160]{2,1,0:T(8,128)S(1)}, f32[6,32,160]{2,1,0:T(8,128)}, u32[]{:S(2)}) copy-start(f32[6,32,160]{2,1,0:T(8,128)} %param.4) | copy-start | bytes 368644
  81.5 178.6 %all-reduce.2.cloned.1.call-start = ((), (), s32[]{:S(2)}) async-start(), calls=%async_computation.3 | async-start | bytes 589824 | tf_op jit(solution)/shard_map/psum | solution.py:64
  113.8 210.0 %all-gather.5.cloned.1.call-start = ((), (), s32[]{:S(2)}) async-start(), calls=%async_computation.4 | async-start | bytes 2785280 | tf_op jit(solution)/shard_map/all_gather | solution.py:55
  113.9 27.0 %collective-permute-start.1 = (f32[192,160]{0,1:T(8,128)}, f32[192,160]{0,1:T(8,128)S(1)}, u32[]{:S(2)}, u32[]{:S(2)}) collective-permute-start(f32[192,160]{0,1:T(8,128)} %reduce-scatter.2.cloned.1.call-done), channel_id=1, source_target_pairs={{0,0},{1,8},{2,16},{3,24},{4,32},{5,40},{6,48},{7,56},{8,64},{9,72... | collective-permute-start | bytes 368648 | tf_op jit(solution)/shard_map/ppermute | solution.py:55
  140.9 0.7 copy-start.4
  277.0 0.8 copy-start.6
  286.8 0.6 copy-start.3
  297.7 12.6 %copy-start.2 = (f32[192,160]{0,1:T(8,128)S(1)}, f32[192,160]{0,1:T(8,128)}, u32[]{:S(2)}) copy-start(f32[192,160]{0,1:T(8,128)} %reduce-scatter.2.cloned.1.call-done) | copy-start | bytes 368644
  320.3 3.4 copy-start
Sparse Core Ops, SparseCore 0:
  18.1 53.3 all-gather.2
  81.6 29.9 reduce-scatter.1
  116.9 143.0 all-reduce.1
  262.0 44.4 all-gather.4

commit v2 on v0

v2 whole, which is shorter than its diff:
```python
import functools

import jax
import jax.numpy as jnp
from jax import lax
from jax.experimental import pallas as pl
from jax.experimental.pallas import tpu as pltpu
from jax.sharding import PartitionSpec as P

HIGHEST = lax.Precision.HIGHEST
MESH = pl.DeviceIdType.MESH
SIDE = 4


class Place:
    def __init__(self):
        pr, pc = lax.axis_index("pr"), lax.axis_index("pc")
        self.x, self.z = lax.rem(pr, SIDE), lax.div(pr, SIDE)
        self.y, self.core = lax.div(pc, 2), lax.rem(pc, 2)

    def at(self, x=0, y=0, z=0, other_core=False):
        far_x = lax.rem(self.x + x + SIDE, SIDE)
        far_y = lax.rem(self.y + y + SIDE, SIDE)
        far_z = lax.rem(self.z + z + SIDE, SIDE)
        core = 1 - self.core if other_core else self.core
        return far_z * SIDE + far_x, far_y * 2 + core

    def spread_to(self):
        block = lax.div(self.x, 2)
        keep = jnp.where(self.core == block, 1, 0)
        far_x = keep * self.x + (1 - keep) * (SIDE - 1 - self.x)
        return self.y * SIDE + far_x, self.z * 2 + block

    def spread_slot(self):
        block = lax.div(self.x, 2)
        return (self.x - 2 * block) * 8 + 2 * self.y + self.core

    def spread_from(self):
        keep = jnp.where(lax.div(self.x, 2) == self.core, 1, 0)
        far_x = keep * self.x + (1 - keep) * (SIDE - 1 - self.x)
        core = keep * self.core + (1 - keep) * (1 - self.core)
        return self.y * SIDE + far_x, self.z * 2 + core

    def column_slot(self, x=0, z=0):
        far_x = lax.rem(self.x + x + SIDE, SIDE)
        far_z = lax.rem(self.z + z + SIDE, SIDE)
        keep = jnp.where(lax.div(far_x, 2) == self.core, 1, 0)
        from_x = keep * far_x + (1 - keep) * (SIDE - 1 - far_x)
        core = keep * self.core + (1 - keep) * (1 - self.core)
        return (from_x - 2 * self.core) * 8 + 2 * far_z + core

    def row_slot(self, y=0, other_core=False):
        core = 1 - self.core if other_core else self.core
        return lax.rem(self.y + y + SIDE, SIDE) * 2 + core


class Mail:
    def __init__(self, send_sem, recv_sem):
        self.send_sem, self.recv_sem = send_sem, recv_sem
        self.count, self.sent = 0, []

    def number(self):
        self.count += 1
        return self.count - 1

    def copy(self, number, source, target, device):
        return pltpu.make_async_remote_copy(
            src_ref=source,
            dst_ref=target,
            send_sem=self.send_sem.at[number],
            recv_sem=self.recv_sem.at[number],
            device_id=device,
            device_id_type=MESH,
        )

    def send(self, number, source, target, device):
        copy = self.copy(number, source, target, device)
        copy.start()
        self.sent.append(copy)

    def receive(self, number, landed, device):
        self.copy(number, landed, landed, device).wait_recv()

    def finish(self):
        for copy in self.sent:
            copy.wait_send()


def is_here(device, place):
    pr, pc = place.at()
    return jnp.logical_and(device[0] == pr, device[1] == pc)


def spans(rows):
    half = rows // 2
    cut = -(-half // 16) * 8
    first, second = pl.ds(0, half), pl.ds(half, half)
    return (
        first,
        second,
        (pl.ds(0, cut), pl.ds(cut, half - cut)),
        (pl.ds(half, cut), pl.ds(half + cut, half - cut)),
    )


def gather(place, mail, own, row, col, local_sem):
    rows = own.shape[0]
    first, second, first_cut, second_cut = spans(rows)
    whole = pl.ds(0, rows)
    target = place.spread_to()
    stays = is_here(target, place)
    spread = mail.number()
    mine = place.column_slot()

    @pl.when(jnp.logical_not(stays))
    def _():
        mail.copy(spread, own, col.at[place.spread_slot()], target).start()

    @pl.when(stays)
    def _():
        pltpu.make_async_copy(own, col.at[mine], local_sem.at[0]).start()

    keep = pltpu.make_async_copy(own, row.at[place.row_slot()], local_sem.at[1])
    keep.start()

    up, down, up_on, down_on = (mail.number() for _ in range(4))
    cross = [mail.number() for _ in range(4)]
    partner = place.at(other_core=True)
    near_up, near_down = place.at(y=1), place.at(y=-1)
    here = place.row_slot()
    mail.send(up, own, row.at[here], near_up)
    mail.send(down, own, row.at[here], near_down)
    mail.send(cross[0], own, row.at[here], partner)

    def row_near():
        below, above = place.row_slot(y=-1), place.row_slot(y=1)
        mail.receive(up, row.at[below], near_down)
        mail.send(up_on, row.at[below, first], row.at[below, first], near_up)
        mail.send(cross[1], row.at[below], row.at[below], partner)
        mail.receive(down, row.at[above], near_up)
        mail.send(down_on, row.at[above, second], row.at[above, second], near_down)
        mail.send(cross[2], row.at[above], row.at[above], partner)

    def row_far():
        far = place.row_slot(y=2)
        mail.receive(up_on, row.at[far, first], near_down)
        mail.receive(down_on, row.at[far, second], near_up)
        mail.send(cross[3], row.at[far], row.at[far], partner)

    def row_end():
        for number, y in ((0, 0), (1, -1), (2, 1), (3, 2)):
            mail.receive(cross[number], row.at[place.row_slot(y=y, other_core=True)], partner)
        keep.wait()

    numbers = {}

    def number(*key):
        if key not in numbers:
            numbers[key] = mail.number()
        return numbers[key]

    def to(axis, step):
        return place.at(**{axis: step})

    def slot(axis, along, across):
        return place.column_slot(x=along, z=across) if axis == "x" else place.column_slot(x=across, z=along)

    def push(axis, step, half, across, span, along=0):
        ref = col.at[slot(axis, along, across), span]
        mail.send(number(axis, step, half, across, along), ref, ref, to(axis, step))

    def pull(axis, step, half, across, span, along=0):
        ref = col.at[slot(axis, along - step, across), span]
        mail.receive(number(axis, step, half, across, along), ref, to(axis, -step))

    halves = {"x": (first, first_cut), "z": (second, second_cut)}
    other = {"x": "z", "z": "x"}

    def start_column():
        @pl.when(jnp.logical_not(stays))
        def _():
            mail.copy(spread, own, col.at[mine], place.spread_from()).wait_recv()

        @pl.when(stays)
        def _():
            pltpu.make_async_copy(own, col.at[mine], local_sem.at[0]).wait()

        for axis in ("x", "z"):
            for step in (1, -1):
                push(axis, step, axis, 0, halves[axis][0])
        for axis in ("x", "z"):
            for step in (1, -1):
                push(axis, step, other[axis], 0, halves[other[axis]][0])

    def first_ring():
        for step, part in ((1, 0), (-1, 1)):
            for axis in ("x", "z"):
                span, cut = halves[axis]
                pull(axis, step, axis, 0, span)
                push(axis, step, axis, 0, cut[part], along=-step)
                for way in (1, -1):
                    push(other[axis], way, axis, -step, span)

    def second_ring_own():
        for step, part in ((1, 0), (-1, 1)):
            for axis in ("x", "z"):
                half = other[axis]
                span, cut = halves[half]
                pull(axis, step, half, 0, span)
                push(axis, step, half, 0, cut[part], along=-step)

    def first_ring_far():
        for axis in ("x", "z"):
            span, cut = halves[axis]
            for step, part in ((1, 0), (-1, 1)):
                pull(axis, step, axis, 0, cut[part], along=-step)
            for way in (1, -1):
                push(other[axis], way, axis, 2, span)

    def second_ring(across):
        for step, part in ((1, 0), (-1, 1)):
            for axis in ("x", "z"):
                half = other[axis]
                span, cut = halves[half]
                pull(axis, step, half, across, span)
                push(axis, step, half, across, cut[part], along=-step)

    def last():
        for across in (0, -1, 1, 2):
            for step, part in ((1, 0), (-1, 1)):
                for axis in ("x", "z"):
                    half = other[axis]
                    pull(axis, step, half, across, halves[half][1][part], along=-step)

    def finish():
        @pl.when(jnp.logical_not(stays))
        def _():
            mail.copy(spread, own, col.at[mine], target).wait_send()

    return {
        "row_near": row_near,
        "start_column": start_column,
        "first_ring": first_ring,
        "second_ring_own": second_ring_own,
        "row_far": row_far,
        "first_ring_far": first_ring_far,
        "second_ring_behind": functools.partial(second_ring, -1),
        "second_ring_ahead": functools.partial(second_ring, 1),
        "second_ring_far": functools.partial(second_ring, 2),
        "row_end": row_end,
        "last": last,
        "finish": finish,
    }


def enter(place, far):
    barrier = pltpu.get_barrier_semaphore()
    near = [place.at(x=1), place.at(x=-1), place.at(z=1), place.at(z=-1), place.at(y=1), place.at(y=-1)]
    near.append(place.at(other_core=True))
    if far:
        near += [place.at(x=2), place.at(y=2), place.at(z=2)]
    target, source = place.spread_to(), place.spread_from()
    moves = jnp.logical_not(is_here(target, place))
    for device in near:
        pl.semaphore_signal(barrier, inc=1, device_id=device, device_id_type=MESH)

    @pl.when(moves)
    def _():
        for device in (target, source):
            pl.semaphore_signal(barrier, inc=1, device_id=device, device_id_type=MESH)

    pl.semaphore_wait(barrier, len(near) + jnp.where(moves, 2, 0))


ORDER = (
    "start_column",
    "row_near",
    "first_ring",
    "second_ring_own",
    "row_far",
    "first_ring_far",
    "second_ring_behind",
    "second_ring_ahead",
    "second_ring_far",
    "row_end",
    "last",
    "finish",
)


def gather_kernel(own, row, col, send_sem, recv_sem, local_sem):
    place = Place()
    enter(place, False)
    mail = Mail(send_sem, recv_sem)
    steps = gather(place, mail, own, row, col, local_sem)
    for name in ORDER:
        steps[name]()
    mail.finish()


def hand_round(own):
    rows, lanes = own.shape
    return pl.pallas_call(
        gather_kernel,
        out_shape=(
            jax.ShapeDtypeStruct((8, rows, lanes), own.dtype),
            jax.ShapeDtypeStruct((16, rows, lanes), own.dtype),
        ),
        in_specs=[pl.BlockSpec(memory_space=pltpu.VMEM)],
        out_specs=[pl.BlockSpec(memory_space=pltpu.VMEM)] * 2,
        scratch_shapes=[
            pltpu.SemaphoreType.DMA((64,)),
            pltpu.SemaphoreType.DMA((64,)),
            pltpu.SemaphoreType.DMA((2,)),
        ],
        compiler_params=pltpu.CompilerParams(collective_id=0, has_side_effects=True),
        name="hand_round",
    )(own)


def total_kernel(partial_ref, grams_ref, row, col, total_ref, swap, sums, near, grams_swap, grams_sum, grams_y, grams_x, grams_z, send_sem, recv_sem, local_sem, own):
    place = Place()
    enter(place, True)
    mail = Mail(send_sem, recv_sem)
    rows = own.shape[0]
    first, second = pl.ds(0, rows // 2), pl.ds(rows // 2, rows // 2)
    partner = place.at(other_core=True)
    near_up, near_down = place.at(y=1), place.at(y=-1)

    half = grams_ref.shape[0] // 2
    part = half // SIDE
    cores = mail.number()
    mail.send(cores, grams_ref.at[pl.ds((1 - place.core) * half, half)], grams_swap, partner)
    across = {y: mail.number() for y in (2, 1, -1, 0)}
    for y, number in across.items():
        mail.send(number, partial_ref.at[place.row_slot(y=y, other_core=True)], swap.at[y % SIDE], partner)

    mail.receive(cores, grams_swap, partner)
    mine = pl.ds(pl.multiple_of(place.core * half, 8), half)
    grams_sum[pl.ds(0, half), :] = grams_ref[mine, :] + grams_swap[...]

    def exchange(axis, source, landing):
        numbers = [mail.number() for _ in range(1, SIDE)]
        for step in range(1, SIDE):
            mail.send(numbers[step - 1], source(step), landing.at[step - 1], place.at(**{axis: step}))

        def arrived():
            for step in range(1, SIDE):
                mail.receive(numbers[step - 1], landing.at[step - 1], place.at(**{axis: -step}))
            return landing[0] + landing[1] + landing[2]

        return arrived

    def quarter(step):
        return pl.ds(pl.multiple_of(lax.rem(place.y + step, SIDE) * part, 8), part)

    over_y = exchange("y", lambda step: grams_sum.at[quarter(step)], grams_y)

    def add_across(y):
        slot = y % SIDE
        mail.receive(across[y], swap.at[slot], partner)
        sums[slot, :, :] = partial_ref[place.row_slot(y=y)] + swap[slot]

    far_up, far_down, up_now, up_later, down_now, down_later = (mail.number() for _ in range(6))
    add_across(2)
    mail.send(far_up, sums.at[2, first], near.at[0, first], near_up)
    mail.send(far_down, sums.at[2, second], near.at[0, second], near_down)
    add_across(1)
    mail.send(up_now, sums.at[1, second], near.at[1, second], near_up)
    add_across(-1)
    mail.send(down_now, sums.at[3, first], near.at[2, first], near_down)
    add_across(0)
    grams_sum[pl.ds(half, part), :] = grams_sum[quarter(0), :] + over_y()
    over_x = exchange("x", lambda step: grams_sum.at[pl.ds(half, part)], grams_x)
    mail.receive(far_up, near.at[0, first], near_down)
    sums[1, first, :] = sums[1, first, :] + near[0, first, :]
    mail.send(up_later, sums.at[1, first], near.at[1, first], near_up)
    mail.receive(far_down, near.at[0, second], near_up)
    sums[3, second, :] = sums[3, second, :] + near[0, second, :]
    mail.send(down_later, sums.at[3, second], near.at[2, second], near_down)
    grams_sum[pl.ds(half + part, part), :] = grams_sum[pl.ds(half, part), :] + over_x()
    over_z = exchange("z", lambda step: grams_sum.at[pl.ds(half + part, part)], grams_z)
    mail.receive(up_now, near.at[1, second], near_down)
    mail.receive(down_now, near.at[2, first], near_up)
    mail.receive(up_later, near.at[1, first], near_down)
    mail.receive(down_later, near.at[2, second], near_up)
    own[...] = sums[0] + near[1] + near[2]

    steps = gather(place, mail, own, row, col, local_sem)

    def total_rows(y, other_core=False):
        core = 1 - place.core if other_core else place.core
        start = core * half + lax.rem(place.y + y + SIDE, SIDE) * part
        return total_ref.at[pl.ds(pl.multiple_of(start, 8), part)]

    start = place.core * half + place.y * part
    total_ref[pl.ds(pl.multiple_of(start, 8), part), :] = grams_sum[pl.ds(half + part, part), :] + over_z()
    back_y = [mail.number() for _ in range(1, SIDE)]
    back_core = [mail.number() for _ in range(SIDE)]
    for step in range(1, SIDE):
        mail.send(back_y[step - 1], total_rows(0), total_rows(0), place.at(y=step))
    mail.send(back_core[0], total_rows(0), total_rows(0), partner)

    def totals_on():
        for step in range(1, SIDE):
            mail.receive(back_y[step - 1], total_rows(-step), place.at(y=-step))
            mail.send(back_core[step], total_rows(-step), total_rows(-step), partner)

    def totals_end():
        for step in range(SIDE):
            mail.receive(back_core[step], total_rows(-step, True), partner)

    for name in ORDER:
        if name == "row_near":
            totals_on()
        if name == "row_far":
            totals_end()
        steps[name]()
    mail.finish()


def total_and_hand_round(partial, grams):
    _, rows, lanes = partial.shape
    parts = grams.shape[0] // 8
    f32 = jnp.float32
    return pl.pallas_call(
        total_kernel,
        out_shape=(
            jax.ShapeDtypeStruct((8, rows, lanes), f32),
            jax.ShapeDtypeStruct((16, rows, lanes), f32),
            jax.ShapeDtypeStruct(grams.shape, f32),
        ),
        in_specs=[pl.BlockSpec(memory_space=pltpu.VMEM)] * 2,
        out_specs=[pl.BlockSpec(memory_space=pltpu.VMEM)] * 3,
        scratch_shapes=[
            pltpu.VMEM((SIDE, rows, lanes), f32),
            pltpu.VMEM((SIDE, rows, lanes), f32),
            pltpu.VMEM((3, rows, lanes), f32),
            pltpu.VMEM((SIDE * parts, lanes), f32),
            pltpu.VMEM((6 * parts, lanes), f32),
            pltpu.VMEM((3, parts, lanes), f32),
            pltpu.VMEM((3, parts, lanes), f32),
            pltpu.VMEM((3, parts, lanes), f32),
            pltpu.SemaphoreType.DMA((96,)),
            pltpu.SemaphoreType.DMA((96,)),
            pltpu.SemaphoreType.DMA((2,)),
            pltpu.VMEM((rows, lanes), f32),
        ],
        compiler_params=pltpu.CompilerParams(collective_id=1, has_side_effects=True),
        name="total_and_hand_round",
    )(partial, grams)


def contract(left_side, right_side, left_dim, right_dim, precision=HIGHEST):
    return lax.dot_general(
        left_side,
        right_side,
        (((left_dim,), (right_dim,)), ((), ())),
        precision=precision,
        preferred_element_type=jnp.float32,
    )


WIDE = 256


def coefficients_kernel(panels, width, of_y_ref, of_v_ref, factor_ref, of_w_ref):
    for panel in range(panels):
        start = panel * width
        here = pl.ds(start, width)
        of_x = of_y_ref[here, :]
        if panel:
            before = pl.ds(0, start)
            of_x = of_x - contract(of_w_ref[before, here], of_v_ref[before, :], 0, 0)
            of_x = of_x - contract(of_v_ref[before, here], of_w_ref[before, :], 0, 0)
        factor = factor_ref[panel]
        scaled = contract(factor, of_x, 0, 0)
        middle = contract(scaled[:, start : start + width], factor, 1, 0)
        of_w_ref[here, :] = scaled - 0.5 * contract(middle, of_v_ref[here, :], 1, 0)


def coefficients(gram_y, gram_v, t_panels):
    panels, width, _ = t_panels.shape
    size = panels * width
    eye = jnp.eye(size, WIDE, dtype=jnp.float32)
    zero = jnp.zeros((size, WIDE), jnp.float32)

    def wide(block):
        return jnp.pad(block, ((0, 0), (0, WIDE - size)))

    of_w = pl.pallas_call(
        functools.partial(coefficients_kernel, panels, width),
        out_shape=jax.ShapeDtypeStruct((size, 3 * WIDE), jnp.float32),
        in_specs=[pl.BlockSpec(memory_space=pltpu.VMEM)] * 3,
        out_specs=pl.BlockSpec(memory_space=pltpu.VMEM),
        name="coefficients",
    )(
        jnp.concatenate([wide(gram_y), zero, eye], axis=1),
        jnp.concatenate([wide(gram_v), eye, zero], axis=1),
        t_panels,
    )
    return of_w[:, WIDE : WIDE + size], of_w[:, 2 * WIDE : 2 * WIDE + size]


def pack(share):
    rows = share.shape[-2] // 2
    tail = share[..., 128:]
    tail = jnp.concatenate([tail[..., :rows, :], tail[..., rows:, :]], axis=-1)
    return jnp.concatenate([share[..., :128], tail], axis=-2)


def unpack(packed):
    rows = packed.shape[-2] // 3
    tail = packed[..., 2 * rows :, :]
    tail = jnp.concatenate([tail[..., :64], tail[..., 64:]], axis=-2)
    return jnp.concatenate([packed[..., : 2 * rows, :], tail], axis=-1)


def per_device(trailing, v_panels, t_panels):
    panels, width, share = v_panels.shape
    size = panels * width
    v_own = v_panels.reshape(size, share).T
    v_row, v_col = hand_round(pack(v_own))
    v_row = unpack(v_row).reshape(-1, size)
    v_col = unpack(v_col).reshape(-1, size)
    partial = contract(trailing, v_col, 1, 0, lax.Precision.HIGH)
    grams = jnp.concatenate([contract(v_row, partial, 0, 0), contract(v_own, v_own, 0, 0)], axis=1)
    grams = jnp.concatenate([grams[:, :128], grams[:, 128:256], grams[:, 256:], jnp.zeros((64, 128), jnp.float32)])
    partial = pack(partial.reshape(-1, share, size))
    y_row, y_col, grams = total_and_hand_round(partial, grams)
    grams = jnp.concatenate([grams[:size], grams[size : 2 * size], grams[2 * size : 3 * size]], axis=1)
    of_v, of_y = coefficients(grams[:, :size], grams[:, size:], t_panels)
    me = lax.axis_index("pc")
    y_own = unpack(lax.dynamic_index_in_dim(y_row, me, 0, keepdims=False))
    y_row = unpack(y_row).reshape(-1, size)
    y_col = unpack(y_col).reshape(-1, size)
    w_own = contract(of_v, v_own, 1, 1) + contract(of_y, y_own, 1, 1)
    left_v = contract(v_row, of_v + of_v.T, 1, 0) + contract(y_row, of_y, 1, 1)
    left_y = contract(v_row, of_y, 1, 0)
    left = jnp.concatenate([left_v, left_y], axis=1)
    right = jnp.concatenate([v_col, y_col], axis=1)
    matrix = trailing - contract(left, right, 1, 1, lax.Precision.HIGH)
    return (matrix, w_own.reshape(panels, width, share))


def solution(mesh):
    return jax.shard_map(
        per_device,
        mesh=mesh,
        in_specs=(P("pr", "pc"), P(None, None, ("pr", "pc")), P()),
        out_specs=(P("pr", "pc"), P(None, None, ("pr", "pc"))),
        check_vma=False,
    )
```

time: 1620 us -> 154 us (0.10)
  the two profiles are of different devices: /device:TPU:1 before, /device:TPU:0 now
where the time goes in v2:
time: 154 us
  Pallas kernels  88.2 us (57%)
  matrix products  40.1 us (26%)
  local copies, waits for them, and re-layouts  18.2 us (12%)
  other arithmetic  6.2 us (4%)
    pallas_call x1, Pallas kernels, total_and_hand_round(): pl.pallas_call(total_kernel, out_shape=(jax.ShapeDtypeStruct((8, rows, la...  44.9 us
    dot_general x9, matrix products, contract(): lax.dot_general(left_side, right_side, (((left_dim,), (right_dim,)), ((),...  40.1 us
    pallas_call x1, Pallas kernels, hand_round(): pl.pallas_call(gather_kernel, out_shape=(jax.ShapeDtypeStruct((8, rows, l...  35.6 us
    pallas_call x1, Pallas kernels, coefficients(): pl.pallas_call(functools.partial(coefficients_kernel, panels, width), out...  7.64 us
    unnamed x26, local copies, waits for them, and re-layouts  7.16 us

profile of v2, /device:TPU:0, one launch (start us, length us, event | category | flops | bytes accessed | tf_op | source)
XLA Modules:
  0.0 153.6 jit_solution(18408544646291998435)
XLA Ops:
  0.6 0.1 pad.35.clone
  0.7 1.0 copy.9
  1.8 0.7 maximum_maximum_fusion.5.own
  2.5 1.4 fusion.35
  3.9 0.1 slice.161
  4.0 35.6 %hand_round.1 = (f32[8,240,128]{2,1,0:T(8,128)}, f32[16,240,128]{2,1,0:T(8,128)}) custom-call(f32[240,128]{1,0:T(8,128)} %maximum_maximum_fusion.5.own), custom_call_target="tpu_custom_call" | custom-call | tf_op jit(solution)/shard_map/hand_round/pallas_call | solution.py:303
  39.7 0.0 copy-start.5
  39.7 1.3 slice.124
  40.9 1.2 fusion.29
  42.2 0.0 copy-start
  42.2 0.1 maximum_maximum_fusion.2
  42.3 0.0 copy-done.5
  42.3 0.1 slice.127
  42.4 0.2 fusion.26
  42.7 0.2 maximum_maximum_fusion
  42.9 0.0 copy-start.1
  42.9 4.9 %copy-done = f32[1280,2560]{1,0:T(8,128)S(1)} copy-done((f32[1280,2560]{1,0:T(8,128)S(1)}, f32[1280,2560]{1,0:T(8,128)}, u32[]{:S(2)}) %copy-start) | copy-done | bytes 13107224
  47.8 11.0 %fusion.33 = f32[192,1280]{1,0:T(8,128)S(1)} fusion(f32[2560,192]{1,0:T(8,128)S(1)} %bitcast.28, f32[1280,2560]{1,0:T(8,128)S(1)} %copy-done), kind=kOutput, calls=%fused_computation.52 | convolution fusion | flops 3774873600 | bytes 16056320 | tf_op jit(solution)/shard_map/dot_general | solution.py:455
  58.8 0.0 copy-done.1
  58.8 2.4 %fusion.34 = f32[192,192]{1,0:T(8,128)S(1)} fusion(f32[1280,192]{1,0:T(8,128)S(1)} %bitcast.30, f32[192,1280]{1,0:T(8,128)S(1)} %fusion.33), kind=kOutput, calls=%fused_computation.53 | convolution fusion | flops 566231040 | bytes 2113536 | tf_op jit(solution)/shard_map/dot_general | solution.py:455
  61.3 0.9 fusion.8.grams_ref
  62.2 1.5 copy.10
  63.7 0.0 copy-start.3
  63.7 1.2 slice.157
  64.9 0.3 copy-done.3
  65.2 1.1 maximum_maximum_fusion.4.partial_ref
  66.3 0.0 copy-start.8
  66.3 44.9 %total_and_hand_round.1 = (f32[8,240,128]{2,1,0:T(8,128)}, f32[16,240,128]{2,1,0:T(8,128)}, f32[640,128]{1,0:T(8,128)}) custom-call(f32[8,240,128]{2,1,0:T(8,128)} %maximum_maximum_fusion.4.partial_ref, f32[640,128]{1,0:T(8,128)} %fusion.8.grams_ref), custom_call_target="tpu_custom_call" | custom-call | tf_op jit(solution)/shard_map/total_and_hand_round/pallas_call | solution.py:426
  111.2 1.0 fusion.30
  112.2 0.8 dynamic-slice_bitcast_fusion.1
  113.0 0.1 fusion.32
  113.1 0.9 dynamic-slice_bitcast_fusion
  114.0 0.0 copy-done.8
  114.0 0.1 select_maximum_fusion
  114.2 1.1 pad_maximum_fusion.1
  115.3 0.0 copy-start.6
  115.3 7.6 %coefficients.1 = f32[192,768]{1,0:T(8,128)} custom-call(f32[192,768]{1,0:T(8,128)} %get-tuple-element.25.of_y_ref, f32[192,768]{1,0:T(8,128)} %get-tuple-element.24.of_v_ref, f32[6,32,32]{2,1,0:T(8,128)} %factor_ref.1), custom_call_target="tpu_custom_call" | custom-call | tf_op jit(solution)/shard_map/coefficients/pallas_call | solution.py:491
  122.9 0.0 slice-start.4
  122.9 1.4 fusion.11
  124.3 0.0 copy-done.6
  124.3 1.5 convolution_add_fusion.1
  125.8 0.8 copy.12
  126.6 0.0 slice-done.4
  126.6 0.1 copy.11
  126.7 0.0 copy-done.7
  126.8 0.0 copy-start.2
  126.8 0.2 fusion.28
  127.0 0.0 slice-start.1
  127.0 0.1 maximum_maximum_fusion.3
  127.1 0.8 copy-done.2
  127.9 1.2 fusion.9
  129.0 0.0 slice-start.2
  129.1 2.3 %convolution_add_fusion = f32[1280,192]{1,0:T(8,128)} fusion(f32[1280,192]{1,0:T(8,128)S(1)} %fusion.9, f32[1280,192]{1,0:T(8,128)S(1)} %bitcast.35, f32[192,768]{1,0:T(8,128)S(1)} %copy-done.2), kind=kOutput, calls=%fused_computation.4 | convolution fusion | flops 566476800 | bytes 3801088 | tf_op jit(solution)/shard_map/dot_general | solution.py:455
  131.4 2.3 %fusion.13 = f32[1280,192]{1,0:T(8,128)} fusion(f32[1280,192]{1,0:T(8,128)S(1)} %bitcast.32, f32[192,768]{1,0:T(8,128)S(1)} %copy-done.2), kind=kOutput, calls=%fused_computation.29 | convolution fusion | flops 566231040 | bytes 2490368 | tf_op jit(solution)/shard_map/dot_general | solution.py:455
  133.6 0.0 copy-done.4
  133.6 0.1 slice.145
  133.7 0.0 slice-start.3
  133.8 0.2 fusion.25
  134.0 1.8 %maximum_maximum_fusion.1 = f32[16,160,192]{2,1,0:T(8,128)} fusion(f32[16,80,64]{2,1,0:T(8,128)S(1)} %get-tuple-element.15, f32[16,80,64]{2,1,0:T(8,128)S(1)} %get-tuple-element.14, f32[16,160,128]{2,1,0:T(8,128)S(1)} %slice.145), kind=kLoop, calls=%fused_computation.6 | loop fusion | flops 983040 | bytes 3932160 | tf_op jit(solution)/shard_map/concatenate | solution.py:516
  135.8 0.0 slice-done
  135.8 0.0 slice-done.1
  135.8 0.0 slice-done.2
  135.8 1.1 slice-done.3
  136.9 16.7 %convolution_subtract_fusion = f32[1280,2560]{1,0:T(8,128)} fusion(f32[1280,2560]{1,0:T(8,128)S(1)} %bitcast.27, f32[2560,192]{1,0:T(8,128)} %bitcast.34, f32[2560,192]{1,0:T(8,128)} %bitcast.29, f32[1280,192]{1,0:T(8,128)} %fusion.13, f32[1280,192]{1,0:T(8,128)} %convolution_add_fusion), kind=kOutput, calls=%fused_computation | convolution fusion | flops 7554498560 | bytes 32112640 | tf_op jit(solution)/shard_map/dot_general | solution.py:455
  (12 shorter events, 0.1 us)
Async XLA Ops:
  39.7 2.6 %copy-start.5 = (f32[16,240,128]{2,1,0:T(8,128)S(1)}, f32[16,240,128]{2,1,0:T(8,128)}, u32[]{:S(2)}) copy-start(f32[16,240,128]{2,1,0:T(8,128)} %get-tuple-element.8) | copy-start | bytes 5898244
  42.2 5.7 %copy-start = (f32[1280,2560]{1,0:T(8,128)S(1)}, f32[1280,2560]{1,0:T(8,128)}, u32[]{:S(2)}) copy-start(f32[1280,2560]{1,0:T(8,128)} %param.3) | copy-start | bytes 39321604
  42.9 15.9 %copy-start.1 = (f32[16,160,192]{2,1,0:T(8,128)}, f32[16,160,192]{2,1,0:T(8,128)S(1)}, u32[]{:S(2)}) copy-start(f32[16,160,192]{2,1,0:T(8,128)S(1)} %maximum_maximum_fusion) | copy-start | bytes 5898244
  63.7 1.5 copy-start.3
  66.3 47.7 %copy-start.8 = (pred[256]{0:T(512)(128)(4,1)S(1)}, pred[256]{0:T(512)(128)(4,1)}, u32[]{:S(2)}) copy-start(pred[256]{0:T(512)(128)(4,1)} %constant.5.clone.1) | copy-start | bytes 772
  115.3 9.1 %copy-start.6 = (f32[6,32,160]{2,1,0:T(8,128)S(1)}, f32[6,32,160]{2,1,0:T(8,128)}, u32[]{:S(2)}) copy-start(f32[6,32,160]{2,1,0:T(8,128)} %param.4) | copy-start | bytes 368644
  122.9 3.7 %slice-start.4 = ((f32[192,768]{1,0:T(8,128)}), f32[192,192]{1,0:T(8,128)S(1)}, s32[]{:S(2)}) async-start(f32[192,768]{1,0:T(8,128)} %coefficients.1), calls=%async_computation.4 | async-start | bytes 393216 | tf_op jit(solution)/shard_map/slice | solution.py:502
  122.9 3.8 %copy-start.7 = (f32[8,240,128]{2,1,0:T(8,128)S(1)}, f32[8,240,128]{2,1,0:T(8,128)}, u32[]{:S(2)}) copy-start(f32[8,240,128]{2,1,0:T(8,128)} %get-tuple-element.10) | copy-start | bytes 2949124
  122.9 12.8 %slice-start = ((s8[13107200]{0:T(1024)(128)(4,1)}), s8[524288]{0:T(1024)(128)(4,1)S(1)}, s32[]{:S(2)}) async-start(s8[13107200]{0:T(1024)(128)(4,1)} %bitcast.26), calls=%async_computation | async-start | bytes 1048576
  126.8 1.1 copy-start.2
  127.0 8.8 %slice-start.1 = ((s8[13107200]{0:T(1024)(128)(4,1)}), s8[4194304]{0:T(1024)(128)(4,1)S(1)}, s32[]{:S(2)}) async-start(s8[13107200]{0:T(1024)(128)(4,1)} %bitcast.26), calls=%async_computation.1 | async-start | bytes 8388608
  129.0 6.7 %slice-start.2 = ((s8[13107200]{0:T(1024)(128)(4,1)}), s8[4194304]{0:T(1024)(128)(4,1)S(1)}, s32[]{:S(2)}) async-start(s8[13107200]{0:T(1024)(128)(4,1)} %bitcast.26), calls=%async_computation.2 | async-start | bytes 8388608
  131.3 2.3 %copy-start.4 = (f32[16,240,128]{2,1,0:T(8,128)S(1)}, f32[16,240,128]{2,1,0:T(8,128)}, u32[]{:S(2)}) copy-start(f32[16,240,128]{2,1,0:T(8,128)} %get-tuple-element.11) | copy-start | bytes 5898244
  133.7 3.1 %slice-start.3 = ((s8[13107200]{0:T(1024)(128)(4,1)}), s8[4194304]{0:T(1024)(128)(4,1)S(1)}, s32[]{:S(2)}) async-start(s8[13107200]{0:T(1024)(128)(4,1)} %bitcast.26), calls=%async_computation.3 | async-start | bytes 8388608

commit v3 on v2

--- a/solution.py
+++ b/solution.py
@@ -288,37 +288,233 @@
 )
 
 
-def gather_kernel(own, row, col, send_sem, recv_sem, local_sem):
+HIGH = lax.Precision.HIGH
+BF16 = jnp.bfloat16
+F32 = jnp.float32
+LANES = 128
+WIDE = 2 * LANES
+
+
+def contract(left_side, right_side, left_dim, right_dim, precision=HIGHEST):
+    return lax.dot_general(
+        left_side,
+        right_side,
+        (((left_dim,), (right_dim,)), ((), ())),
+        precision=precision,
+        preferred_element_type=F32,
+    )
+
+
+def split(value):
+    high = value.astype(BF16).astype(F32)
+    return high, value - high
+
+
+def left_lanes(shape):
+    return lax.broadcasted_iota(jnp.int32, shape, len(shape) - 1) < LANES // 2
+
+
+def swap_halves(value):
+    return pltpu.roll(value, LANES // 2, 1)
+
+
+def unpack(packed, wide, start):
+    rows = packed.shape[0] // 3
+    tail = packed[pl.ds(2 * rows, rows), :]
+    left = left_lanes(tail.shape)
+    wide[pl.ds(start, 2 * rows), 0:LANES] = packed[pl.ds(0, 2 * rows), :]
+    wide[pl.ds(start, rows), LANES:WIDE] = jnp.where(left, tail, 0.0)
+    wide[pl.ds(start + rows, rows), LANES:WIDE] = jnp.where(left, swap_halves(tail), 0.0)
+
+
+def unpack_split(packed, parts, start, lane=0):
+    rows = packed.shape[0] // 3
+    high, low = split(packed[pl.ds(0, 2 * rows), :])
+    parts[pl.ds(start, 2 * rows), lane : lane + LANES] = low.astype(BF16)
+    parts[pl.ds(start, 2 * rows), lane + LANES : lane + 2 * LANES] = high.astype(BF16)
+    high, low = split(packed[pl.ds(2 * rows, rows), :])
+    left = left_lanes(high.shape)
+    ends = slice(lane + 2 * LANES, lane + 3 * LANES)
+    parts[pl.ds(start, rows), ends] = jnp.where(left, high, swap_halves(low)).astype(BF16)
+    parts[pl.ds(start + rows, rows), ends] = jnp.where(left, swap_halves(high), low).astype(BF16)
+
+
+CHUNK = 128
+BLOCK = 320
+
+
+def product_kernel(
+    own, matrix, row, right, partial, grams, col, stage, high, low, row_wide, row_flat, product, send_sem, recv_sem, local_sem, stage_sem
+):
     place = Place()
+    rows = own.shape[0]
+    share = 2 * rows // 3
+    chunks = matrix.shape[0] // CHUNK
+
+    def load(chunk):
+        return pltpu.make_async_copy(matrix.at[pl.ds(chunk * CHUNK, CHUNK)], stage.at[chunk % 3], stage_sem.at[chunk % 3])
+
+    for chunk in range(3):
+        load(chunk).start()
     enter(place, False)
     mail = Mail(send_sem, recv_sem)
     steps = gather(place, mail, own, row, col, local_sem)
+    todo = list(range(chunks))
+
+    def convert():
+        chunk = todo.pop(0)
+        load(chunk).wait()
+        top, rest = split(stage[chunk % 3])
+        high[pl.ds(chunk * CHUNK, CHUNK), :] = top.astype(BF16)
+        low[pl.ds(chunk * CHUNK, CHUNK), :] = rest.astype(BF16)
+        if chunk + 3 < chunks:
+            load(chunk + 3).start()
+
+    def row_grams():
+        for slot in range(8):
+            unpack(row.at[slot], row_wide, slot * share)
+        row_flat[...] = row_wide[...].T
+        gram = contract(row_flat[0:192, :], row_wide[...], 1, 0, HIGH) * 0.125
+        grams[384:576, :] = gram[:, 0:LANES]
+        grams[576:768, :] = gram[:, LANES:WIDE]
+
+    convert()
+    convert()
+    convert()
     for name in ORDER:
         steps[name]()
+        if name == "row_end":
+            while todo:
+                convert()
+            row_grams()
+        elif name != "start_column" and todo:
+            convert()
+    for slot in range(16):
+        unpack_split(col.at[slot], right, slot * share)
+
+    @pl.loop(0, matrix.shape[0] // BLOCK)
+    def _(block):
+        here = pl.ds(pl.multiple_of(block * BLOCK, BLOCK), BLOCK)
+        top = jnp.dot(high[here, :], right[...], preferred_element_type=F32)
+        rest = jnp.dot(low[here, :], right[:, LANES:], preferred_element_type=F32)
+        main = top[:, 0:LANES] + top[:, LANES : 2 * LANES] + rest[:, 0:LANES]
+        tail = top[:, 2 * LANES :] + rest[:, LANES:]
+        tail = tail + swap_halves(tail)
+        product[here, 0:LANES] = main
+        product[here, LANES:WIDE] = jnp.where(left_lanes(tail.shape), tail, 0.0)
+        left = left_lanes((share // 2, LANES))
+        for piece in range(BLOCK // share):
+            slot = block * (BLOCK // share) + piece
+            start = piece * share
+            partial[slot, 0:share, :] = main[start : start + share]
+            near, far = tail[start : start + share // 2], tail[start + share // 2 : start + share]
+            partial[slot, share:, :] = jnp.where(left, near, far)
+
+    gram = contract(row_flat[0:192, :], product[...], 1, 0, HIGH)
+    grams[0:192, :] = gram[:, 0:LANES]
+    grams[192:384, :] = gram[:, LANES:WIDE]
     mail.finish()
 
 
-def hand_round(own):
+def in_vmem(count):
+    return [pl.BlockSpec(memory_space=pltpu.VMEM)] * count
+
+
+def product_call(own, matrix):
     rows, lanes = own.shape
+    height, length = matrix.shape
     return pl.pallas_call(
-        gather_kernel,
+        product_kernel,
         out_shape=(
-            jax.ShapeDtypeStruct((8, rows, lanes), own.dtype),
-            jax.ShapeDtypeStruct((16, rows, lanes), own.dtype),
+            jax.ShapeDtypeStruct((8, rows, lanes), F32),
+            jax.ShapeDtypeStruct((length, 3 * LANES), BF16),
+            jax.ShapeDtypeStruct((8, rows, lanes), F32),
+            jax.ShapeDtypeStruct((768, lanes), F32),
         ),
-        in_specs=[pl.BlockSpec(memory_space=pltpu.VMEM)],
-        out_specs=[pl.BlockSpec(memory_space=pltpu.VMEM)] * 2,
+        in_specs=in_vmem(1) + [pl.BlockSpec(memory_space=pl.ANY)],
+        out_specs=in_vmem(4),
         scratch_shapes=[
+            pltpu.VMEM((16, rows, lanes), F32),
+            pltpu.VMEM((3, CHUNK, length), F32),
+            pltpu.VMEM((height, length), BF16),
+            pltpu.VMEM((height, length), BF16),
+            pltpu.VMEM((height, WIDE), F32),
+            pltpu.VMEM((WIDE, height), F32),
+            pltpu.VMEM((height, WIDE), F32),
             pltpu.SemaphoreType.DMA((64,)),
             pltpu.SemaphoreType.DMA((64,)),
             pltpu.SemaphoreType.DMA((2,)),
+            pltpu.SemaphoreType.DMA((3,)),
         ],
-        compiler_params=pltpu.CompilerParams(collective_id=0, has_side_effects=True),
-        name="hand_round",
-    )(own)
-
-
-def total_kernel(partial_ref, grams_ref, row, col, total_ref, swap, sums, near, grams_swap, grams_sum, grams_y, grams_x, grams_z, send_sem, recv_sem, local_sem, own):
+        compiler_params=pltpu.CompilerParams(collective_id=0, has_side_effects=True, vmem_limit_bytes=60 * 1024 * 1024),
+        name="v_shares_and_product",
+    )(own, matrix)
+
+
+def coefficient_steps(panels, width, total_ref, factor_ref, of_y, of_v, of_w):
+    size = panels * width
+
+    def begin():
+        rows = lax.broadcasted_iota(jnp.int32, (size, WIDE), 0)
+        cols = lax.broadcasted_iota(jnp.int32, (size, WIDE), 1)
+        eye = jnp.where(rows == cols, 1.0, 0.0)
+        zero = jnp.zeros((size, WIDE), F32)
+        for ref, first, at in ((of_y, 0, 2), (of_v, 2 * size, 1)):
+            ref[:, 0:LANES] = total_ref[pl.ds(first, size), :]
+            ref[:, LANES:WIDE] = total_ref[pl.ds(first + size, size), :]
+            ref[:, WIDE * at : WIDE * (at + 1)] = eye
+            ref[:, WIDE * (3 - at) : WIDE * (4 - at)] = zero
+
+    def step(panel):
+        start = panel * width
+        here = slice(start, start + width)
+        of_x = of_y[here, :]
+        if panel:
+            before = slice(0, start)
+            of_x = of_x - contract(of_w[before, here], of_v[before, :], 0, 0)
+            of_x = of_x - contract(of_v[before, here], of_w[before, :], 0, 0)
+        factor = factor_ref[panel]
+        scaled = contract(factor, of_x, 0, 0)
+        middle = contract(scaled[:, here], factor, 1, 0)
+        of_w[here, :] = scaled - 0.5 * contract(middle, of_v[here, :], 1, 0)
+
+    return begin, step
+
+
+def total_kernel(
+    panels,
+    width,
+    partial_ref,
+    grams_ref,
+    row_v,
+    right_v,
+    factor_ref,
+    right,
+    left_high,
+    left_low,
+    w_ref,
+    row,
+    col,
+    total_ref,
+    swap,
+    sums,
+    near,
+    grams_swap,
+    grams_sum,
+    grams_y,
+    grams_x,
+    grams_z,
+    own,
+    of_y,
+    of_v,
+    of_w,
+    mixing,
+    share_v,
+    share_y,
+    send_sem,
+    recv_sem,
+    local_sem,
+):
     place = Place()
     enter(place, True)
     mail = Mail(send_sem, recv_sem)
@@ -410,137 +606,165 @@
         for step in range(SIDE):
             mail.receive(back_core[step], total_rows(-step, True), partner)
 
+    begin, step = coefficient_steps(panels, width, total_ref, factor_ref, of_y, of_v, of_w)
+    size = panels * width
+    share = 2 * own.shape[0] // 3
+
+    def mix():
+        mixing[...] = jnp.zeros_like(mixing)
+        of_d, of_c = of_w[:, WIDE : 2 * WIDE], of_w[:, 2 * WIDE :]
+        mixing[0:size, 0:WIDE] = of_d
+        mixing[:, 0:WIDE] = mixing[:, 0:WIDE] + mixing[:, 0:WIDE].T
+        mixing[0:size, WIDE:] = of_c
+
+    def store_left(value, start, lane, low_lane):
+        left = left_lanes((share, LANES))
+        for at in range(2):
+            top, rest = split(value[:, at * LANES : (at + 1) * LANES])
+            if at:
+                top = jnp.where(left, top, swap_halves(top))
+                rest = jnp.where(left, rest, swap_halves(rest))
+            here = pl.ds(start, share)
+            low_here = slice(low_lane + at * LANES, low_lane + (at + 1) * LANES)
+            left_low[here, low_here] = rest.astype(BF16)
+            if not at:
+                left_high[here, lane : lane + LANES] = top.astype(BF16)
+            left_high[here, lane + (at + 1) * LANES : lane + (at + 2) * LANES] = top.astype(BF16)
+
+    def left_rows(slot):
+        unpack(row_v.at[slot], share_v, 0)
+        unpack(row.at[slot], share_y, 0)
+        of_right_v = contract(share_v[...], mixing[:, 0:WIDE], 1, 0, HIGH)
+        of_right_v = of_right_v + contract(share_y[...], mixing[:, WIDE:], 1, 1, HIGH)
+        of_right_y = contract(share_v[...], mixing[:, WIDE:], 1, 0, HIGH)
+        store_left(of_right_v, slot * share, 0, 0)
+        store_left(of_right_y, slot * share, 3 * LANES, 2 * LANES)
+
+    def w_rows():
+        unpack(row_v.at[place.row_slot()], share_v, 0)
+        unpack(own, share_y, 0)
+        w_ref[...] = contract(of_w[:, WIDE : 2 * WIDE], share_v[...], 1, 1, HIGH)
+        w_ref[...] = w_ref[...] + contract(of_w[:, 2 * WIDE :], share_y[...], 1, 1, HIGH)
+
+    after = {
+        "second_ring_own": [begin, lambda: step(0)],
+        "row_far": [lambda: step(1), lambda: step(2)],
+        "first_ring_far": [lambda: step(3)],
+        "second_ring_behind": [lambda: step(4)],
+        "second_ring_ahead": [lambda: step(5), mix],
+        "second_ring_far": [w_rows],
+        "row_end": [functools.partial(left_rows, slot) for slot in range(8)],
+    }
+    right[:, 0 : 3 * LANES] = right_v[...]
     for name in ORDER:
         if name == "row_near":
             totals_on()
-        if name == "row_far":
+        steps[name]()
+        if name == "first_ring":
             totals_end()
-        steps[name]()
+        for work in after.get(name, ()):
+            work()
+    for slot in range(16):
+        unpack_split(col.at[slot], right, slot * share, 3 * LANES)
     mail.finish()
 
 
-def total_and_hand_round(partial, grams):
+def total_call(partial, grams, row_v, right_v, factors):
     _, rows, lanes = partial.shape
+    panels, width, _ = factors.shape
+    size = panels * width
+    share = 2 * rows // 3
+    length = right_v.shape[0]
     parts = grams.shape[0] // 8
-    f32 = jnp.float32
     return pl.pallas_call(
-        total_kernel,
+        functools.partial(total_kernel, panels, width),
         out_shape=(
-            jax.ShapeDtypeStruct((8, rows, lanes), f32),
-            jax.ShapeDtypeStruct((16, rows, lanes), f32),
-            jax.ShapeDtypeStruct(grams.shape, f32),
+            jax.ShapeDtypeStruct((length, 6 * LANES), BF16),
+            jax.ShapeDtypeStruct((8 * share, 6 * LANES), BF16),
+            jax.ShapeDtypeStruct((8 * share, 4 * LANES), BF16),
+            jax.ShapeDtypeStruct((size, share), F32),
         ),
-        in_specs=[pl.BlockSpec(memory_space=pltpu.VMEM)] * 2,
-        out_specs=[pl.BlockSpec(memory_space=pltpu.VMEM)] * 3,
+        in_specs=in_vmem(5),
+        out_specs=in_vmem(4),
         scratch_shapes=[
-            pltpu.VMEM((SIDE, rows, lanes), f32),
-            pltpu.VMEM((SIDE, rows, lanes), f32),
-            pltpu.VMEM((3, rows, lanes), f32),
-            pltpu.VMEM((SIDE * parts, lanes), f32),
-            pltpu.VMEM((6 * parts, lanes), f32),
-            pltpu.VMEM((3, parts, lanes), f32),
-            pltpu.VMEM((3, parts, lanes), f32),
-            pltpu.VMEM((3, parts, lanes), f32),
+            pltpu.VMEM((8, rows, lanes), F32),
+            pltpu.VMEM((16, rows, lanes), F32),
+            pltpu.VMEM(grams.shape, F32),
+            pltpu.VMEM((SIDE, rows, lanes), F32),
+            pltpu.VMEM((SIDE, rows, lanes), F32),
+            pltpu.VMEM((3, rows, lanes), F32),
+            pltpu.VMEM((SIDE * parts, lanes), F32),
+            pltpu.VMEM((6 * parts, lanes), F32),
+            pltpu.VMEM((3, parts, lanes), F32),
+            pltpu.VMEM((3, parts, lanes), F32),
+            pltpu.VMEM((3, parts, lanes), F32),
+            pltpu.VMEM((rows, lanes), F32),
+            pltpu.VMEM((size, 3 * WIDE), F32),
+            pltpu.VMEM((size, 3 * WIDE), F32),
+            pltpu.VMEM((size, 3 * WIDE), F32),
+            pltpu.VMEM((WIDE, 2 * WIDE), F32),
+            pltpu.VMEM((share, WIDE), F32),
+            pltpu.VMEM((share, WIDE), F32),
             pltpu.SemaphoreType.DMA((96,)),
             pltpu.SemaphoreType.DMA((96,)),
             pltpu.SemaphoreType.DMA((2,)),
-            pltpu.VMEM((rows, lanes), f32),
         ],
-        compiler_params=pltpu.CompilerParams(collective_id=1, has_side_effects=True),
-        name="total_and_hand_round",
-    )(partial, grams)
-
-
-def contract(left_side, right_side, left_dim, right_dim, precision=HIGHEST):
-    return lax.dot_general(
-        left_side,
-        right_side,
-        (((left_dim,), (right_dim,)), ((), ())),
-        precision=precision,
-        preferred_element_type=jnp.float32,
-    )
-
-
-WIDE = 256
-
-
-def coefficients_kernel(panels, width, of_y_ref, of_v_ref, factor_ref, of_w_ref):
-    for panel in range(panels):
-        start = panel * width
-        here = pl.ds(start, width)
-        of_x = of_y_ref[here, :]
-        if panel:
-            before = pl.ds(0, start)
-            of_x = of_x - contract(of_w_ref[before, here], of_v_ref[before, :], 0, 0)
-            of_x = of_x - contract(of_v_ref[before, here], of_w_ref[before, :], 0, 0)
-        factor = factor_ref[panel]
-        scaled = contract(factor, of_x, 0, 0)
-        middle = contract(scaled[:, start : start + width], factor, 1, 0)
-        of_w_ref[here, :] = scaled - 0.5 * contract(middle, of_v_ref[here, :], 1, 0)
-
-
-def coefficients(gram_y, gram_v, t_panels):
-    panels, width, _ = t_panels.shape
-    size = panels * width
-    eye = jnp.eye(size, WIDE, dtype=jnp.float32)
-    zero = jnp.zeros((size, WIDE), jnp.float32)
-
-    def wide(block):
-        return jnp.pad(block, ((0, 0), (0, WIDE - size)))
-
-    of_w = pl.pallas_call(
-        functools.partial(coefficients_kernel, panels, width),
-        out_shape=jax.ShapeDtypeStruct((size, 3 * WIDE), jnp.float32),
-        in_specs=[pl.BlockSpec(memory_space=pltpu.VMEM)] * 3,
-        out_specs=pl.BlockSpec(memory_space=pltpu.VMEM),
-        name="coefficients",
-    )(
-        jnp.concatenate([wide(gram_y), zero, eye], axis=1),
-        jnp.concatenate([wide(gram_v), eye, zero], axis=1),
-        t_panels,
-    )
-    return of_w[:, WIDE : WIDE + size], of_w[:, 2 * WIDE : 2 * WIDE + size]
+        compiler_params=pltpu.CompilerParams(collective_id=1, has_side_effects=True, vmem_limit_bytes=60 * 1024 * 1024),
+        name="totals_and_factors",
+    )(partial, grams, row_v, right_v, factors)
+
+
+TILE = 256
+
+
+def update_kernel(matrix_ref, right_ref, high_ref, low_ref, w_in, out_ref, w_out):
+    right = right_ref[...]
+    change = contract(high_ref[...], right, 1, 1, None)
+    low_v, low_y = low_ref[:, 0 : 2 * LANES], low_ref[:, 2 * LANES :]
+    change = change + contract(low_v, right[:, LANES : 3 * LANES], 1, 1, None)
+    change = change + contract(low_y, right[:, 4 * LANES :], 1, 1, None)
+    out_ref[...] = matrix_ref[...] - change
+    w_out[...] = w_in[...]
+
+
+def update_call(matrix, right, left_high, left_low, w):
+    height, length = matrix.shape
+
+    def whole(array):
+        return pl.BlockSpec(array.shape, lambda tile: (0, 0), pipeline_mode=pl.Buffered(1))
+
+    return pl.pallas_call(
+        update_kernel,
+        grid=(length // TILE,),
+        out_shape=(jax.ShapeDtypeStruct(matrix.shape, F32), jax.ShapeDtypeStruct(w.shape, F32)),
+        in_specs=[
+            pl.BlockSpec((height, TILE), lambda tile: (0, tile)),
+            pl.BlockSpec((TILE, right.shape[1]), lambda tile: (tile, 0)),
+            whole(left_high),
+            whole(left_low),
+            whole(w),
+        ],
+        out_specs=[pl.BlockSpec((height, TILE), lambda tile: (0, tile)), pl.BlockSpec(w.shape, lambda tile: (0, 0))],
+        compiler_params=pltpu.CompilerParams(dimension_semantics=("arbitrary",), vmem_limit_bytes=60 * 1024 * 1024),
+        name="update",
+    )(matrix, right, left_high, left_low, w)
 
 
 def pack(share):
-    rows = share.shape[-2] // 2
-    tail = share[..., 128:]
-    tail = jnp.concatenate([tail[..., :rows, :], tail[..., rows:, :]], axis=-1)
-    return jnp.concatenate([share[..., :128], tail], axis=-2)
-
-
-def unpack(packed):
-    rows = packed.shape[-2] // 3
-    tail = packed[..., 2 * rows :, :]
-    tail = jnp.concatenate([tail[..., :64], tail[..., 64:]], axis=-2)
-    return jnp.concatenate([packed[..., : 2 * rows, :], tail], axis=-1)
+    rows = share.shape[0] // 2
+    tail = share[:, LANES:]
+    tail = jnp.concatenate([tail[:rows], tail[rows:]], axis=1)
+    return jnp.concatenate([share[:, :LANES], tail], axis=0)
 
 
 def per_device(trailing, v_panels, t_panels):
     panels, width, share = v_panels.shape
     size = panels * width
-    v_own = v_panels.reshape(size, share).T
-    v_row, v_col = hand_round(pack(v_own))
-    v_row = unpack(v_row).reshape(-1, size)
-    v_col = unpack(v_col).reshape(-1, size)
-    partial = contract(trailing, v_col, 1, 0, lax.Precision.HIGH)
-    grams = jnp.concatenate([contract(v_row, partial, 0, 0), contract(v_own, v_own, 0, 0)], axis=1)
-    grams = jnp.concatenate([grams[:, :128], grams[:, 128:256], grams[:, 256:], jnp.zeros((64, 128), jnp.float32)])
-    partial = pack(partial.reshape(-1, share, size))
-    y_row, y_col, grams = total_and_hand_round(partial, grams)
-    grams = jnp.concatenate([grams[:size], grams[size : 2 * size], grams[2 * size : 3 * size]], axis=1)
-    of_v, of_y = coefficients(grams[:, :size], grams[:, size:], t_panels)
-    me = lax.axis_index("pc")
-    y_own = unpack(lax.dynamic_index_in_dim(y_row, me, 0, keepdims=False))
-    y_row = unpack(y_row).reshape(-1, size)
-    y_col = unpack(y_col).reshape(-1, size)
-    w_own = contract(of_v, v_own, 1, 1) + contract(of_y, y_own, 1, 1)
-    left_v = contract(v_row, of_v + of_v.T, 1, 0) + contract(y_row, of_y, 1, 1)
-    left_y = contract(v_row, of_y, 1, 0)
-    left = jnp.concatenate([left_v, left_y], axis=1)
-    right = jnp.concatenate([v_col, y_col], axis=1)
-    matrix = trailing - contract(left, right, 1, 1, lax.Precision.HIGH)
-    return (matrix, w_own.reshape(panels, width, share))
+    own = pack(v_panels.reshape(size, share).T)
+    row_v, right_v, partial, grams = product_call(own, trailing)
+    right, left_high, left_low, w = total_call(partial, grams, row_v, right_v, t_panels)
+    matrix, w = update_call(trailing, right, left_high, left_low, w)
+    return (matrix, w.reshape(panels, width, share))
 
 
 def solution(mesh):

time: 154 us -> 112 us (0.73)
  matrix products: 40.1 us -> 0 us
  Pallas kernels: 88.2 us -> 109 us
  local copies, waits for them, and re-layouts: 18.2 us -> 1.04 us
  other arithmetic: 6.2 us -> 0.73 us
    dot_general x9 -> x0, matrix products: 40.1 us -> none  [contract(): lax.dot_general(left_side, right_side, (((left_dim,), (right_dim,)), ((),...]
    pallas_call x3, Pallas kernels: 88.2 us -> 109 us  [the longest x1 48.1 us: total_call(): pl.pallas_call(functools.partial(total_kernel, panels, width), out_shape=...]
    slice x21 -> x2, local copies, waits for them, and re-layouts: 7.71 us -> 0.02 us  [the longest x1 0.01 us: pack(): tail = jnp.concatenate([tail[:rows], tail[rows:]], axis=1)]
    unnamed x26 -> x0, local copies, waits for them, and re-layouts: 7.16 us -> none
    concatenate x9 -> x1, other arithmetic: 6.18 us -> 0.73 us  [pack(): return jnp.concatenate([share[:, :LANES], tail], axis=0)]
where the time goes in v3:
time: 112 us
  Pallas kernels  109 us (97%)
    pallas_call x1, Pallas kernels, total_call(): pl.pallas_call(functools.partial(total_kernel, panels, width), out_shape=...  48.1 us
    pallas_call x1, Pallas kernels, product_call(): pl.pallas_call(product_kernel, out_shape=(jax.ShapeDtypeStruct((8, rows,...  43.1 us
    pallas_call x1, Pallas kernels, update_call(): pl.pallas_call(update_kernel, grid=(length // TILE,), out_shape=(jax.Shap...  18 us

profile of v3, /device:TPU:0, one launch (start us, length us, event | category | flops | bytes accessed | tf_op | source)
XLA Modules:
  0.0 111.7 jit_solution(2658453790375993448)
XLA Ops:
  0.6 1.0 copy.6
  1.7 0.7 maximum_maximum_fusion.own
  2.4 43.1 %v_shares_and_product.1 = (f32[8,240,128]{2,1,0:T(8,128)}, bf16[2560,384]{1,0:T(8,128)(2,1)}, f32[8,240,128]{2,1,0:T(8,128)}, f32[768,128]{1,0:T(8,128)}) custom-call(f32[240,128]{1,0:T(8,128)} %maximum_maximum_fusion.own, f32[1280,2560]{1,0:T(8,128)} %matrix_ref.1), custom_call_target="tpu_custom_call" | custom-call | tf_op jit(solution)/shard_map/v_shares_and_product/pallas_call | solution.py:426
  45.6 48.1 %totals_and_factors.1 = (bf16[2560,768]{1,0:T(8,128)(2,1)}, bf16[1280,768]{1,0:T(8,128)(2,1)}, bf16[1280,512]{1,0:T(8,128)(2,1)}, f32[192,160]{1,0:T(8,128)}) custom-call(f32[8,240,128]{2,1,0:T(8,128)} %get-tuple-element.12.partial_ref, f32[768,128]{1,0:T(8,128)} %get-tuple-element.13.grams_ref, f32[8,240,128]{2,1,0:T(8,128)} %get-tuple-element.14.row_v, ...), custom_call_target="tpu_custom_call" | custom-call | tf_op jit(solution)/shard_map/totals_and_factors/pallas_call | solution.py:679
  93.6 18.0 %update.1 = (f32[1280,2560]{1,0:T(8,128)}, f32[192,160]{1,0:T(8,128)}) custom-call(f32[1280,2560]{1,0:T(8,128)} %matrix_ref.1, bf16[2560,768]{1,0:T(8,128)(2,1)} %get-tuple-element.16.right_ref, bf16[1280,768]{1,0:T(8,128)(2,1)} %get-tuple-element.17.high_ref, bf16[1280,512]{1,0:T(8,128)(2,1)} %get-tuple-element.18.low_ref, f32[192,160]{1,0:T(8,128)} %get-tuple-element.19.w_in), custom_call_target="tpu_custom_call" | custom-call | tf_op jit(solution)/shard_map/update/pallas_call | solution.py:736
  (2 shorter events, 0.0 us)

commit v4 on v1

v4 whole, which is shorter than its diff:
```python
import functools

import jax
import jax.numpy as jnp
from jax import lax
from jax.experimental import pallas as pl
from jax.experimental.pallas import tpu as pltpu
from jax.sharding import PartitionSpec as P

HIGHEST = lax.Precision.HIGHEST
MESH = pl.DeviceIdType.MESH
SIDE = 4


class Place:
    def __init__(self):
        pr, pc = lax.axis_index("pr"), lax.axis_index("pc")
        self.x, self.z = lax.rem(pr, SIDE), lax.div(pr, SIDE)
        self.y, self.core = lax.div(pc, 2), lax.rem(pc, 2)

    def at(self, x=0, y=0, z=0, other_core=False):
        far_x = lax.rem(self.x + x + SIDE, SIDE)
        far_y = lax.rem(self.y + y + SIDE, SIDE)
        far_z = lax.rem(self.z + z + SIDE, SIDE)
        core = 1 - self.core if other_core else self.core
        return far_z * SIDE + far_x, far_y * 2 + core

    def spread_to(self):
        block = lax.div(self.x, 2)
        keep = jnp.where(self.core == block, 1, 0)
        far_x = keep * self.x + (1 - keep) * (SIDE - 1 - self.x)
        return lax.rem(self.y + self.z, SIDE) * SIDE + far_x, self.z * 2 + block

    def spread_slot(self):
        block = lax.div(self.x, 2)
        return (self.x - 2 * block) * 8 + 2 * self.y + self.core

    def spread_from(self):
        keep = jnp.where(lax.div(self.x, 2) == self.core, 1, 0)
        far_x = keep * self.x + (1 - keep) * (SIDE - 1 - self.x)
        core = keep * self.core + (1 - keep) * (1 - self.core)
        return self.y * SIDE + far_x, lax.rem(self.z - self.y + SIDE, SIDE) * 2 + core

    def column_slot(self, x=0, z=0):
        far_x = lax.rem(self.x + x + SIDE, SIDE)
        far_z = lax.rem(self.z + z + SIDE, SIDE)
        keep = jnp.where(lax.div(far_x, 2) == self.core, 1, 0)
        from_x = keep * far_x + (1 - keep) * (SIDE - 1 - far_x)
        core = keep * self.core + (1 - keep) * (1 - self.core)
        return (from_x - 2 * self.core) * 8 + 2 * lax.rem(far_z - self.y + SIDE, SIDE) + core

    def row_slot(self, y=0, other_core=False):
        core = 1 - self.core if other_core else self.core
        return lax.rem(self.y + y + SIDE, SIDE) * 2 + core


class Mail:
    def __init__(self, send_sem, recv_sem):
        self.send_sem, self.recv_sem = send_sem, recv_sem
        self.count, self.sent = 0, []

    def number(self):
        self.count += 1
        return self.count - 1

    def copy(self, number, source, target, device):
        return pltpu.make_async_remote_copy(
            src_ref=source,
            dst_ref=target,
            send_sem=self.send_sem.at[number],
            recv_sem=self.recv_sem.at[number],
            device_id=device,
            device_id_type=MESH,
        )

    def send(self, number, source, target, device):
        copy = self.copy(number, source, target, device)
        copy.start()
        self.sent.append(copy)

    def receive(self, number, landed, device):
        self.copy(number, landed, landed, device).wait_recv()

    def finish(self):
        for copy in self.sent:
            copy.wait_send()


def is_here(device, place):
    pr, pc = place.at()
    return jnp.logical_and(device[0] == pr, device[1] == pc)


def spans(rows):
    half = rows // 2
    cut = -(-half // 16) * 8
    first, second = pl.ds(0, half), pl.ds(half, half)
    return (
        first,
        second,
        (pl.ds(0, cut), pl.ds(cut, half - cut)),
        (pl.ds(half, cut), pl.ds(half + cut, half - cut)),
    )


class Spread:
    def __init__(self, place, mail, back=False):
        self.mail, self.number = mail, mail.number()
        self.target = place.spread_from() if back else place.spread_to()
        self.source = place.spread_to() if back else place.spread_from()
        self.stays = is_here(self.target, place)

    def start(self, own, landing, landed, local_sem):
        self.own, self.landed = own, landed
        self.local = pltpu.make_async_copy(own, landed, local_sem)
        self.remote = self.mail.copy(self.number, own, landing, self.target)

        @pl.when(jnp.logical_not(self.stays))
        def _():
            self.remote.start()

        @pl.when(self.stays)
        def _():
            self.local.start()

    def arrived(self):
        @pl.when(jnp.logical_not(self.stays))
        def _():
            self.mail.copy(self.number, self.own, self.landed, self.source).wait_recv()

        @pl.when(self.stays)
        def _():
            self.local.wait()

    def finish(self):
        @pl.when(jnp.logical_not(self.stays))
        def _():
            self.remote.wait_send()


class RowRing:
    def __init__(self, place, mail, own, row, local_sem):
        self.place, self.mail, self.own, self.row = place, mail, own, row
        self.first, self.second, _, _ = spans(own.shape[0])
        self.up, self.down, self.up_on, self.down_on = (mail.number() for _ in range(4))
        self.cross = [mail.number() for _ in range(4)]
        self.partner = place.at(other_core=True)
        self.near_up, self.near_down = place.at(y=1), place.at(y=-1)
        self.keep = pltpu.make_async_copy(own, row.at[place.row_slot()], local_sem)

    def start(self):
        here = self.row.at[self.place.row_slot()]
        self.keep.start()
        self.mail.send(self.up, self.own, here, self.near_up)
        self.mail.send(self.down, self.own, here, self.near_down)
        self.mail.send(self.cross[0], self.own, here, self.partner)

    def near(self):
        mail, row = self.mail, self.row
        below, above = self.place.row_slot(y=-1), self.place.row_slot(y=1)
        mail.receive(self.up, row.at[below], self.near_down)
        mail.send(self.up_on, row.at[below, self.first], row.at[below, self.first], self.near_up)
        mail.send(self.cross[1], row.at[below], row.at[below], self.partner)
        mail.receive(self.down, row.at[above], self.near_up)
        mail.send(self.down_on, row.at[above, self.second], row.at[above, self.second], self.near_down)
        mail.send(self.cross[2], row.at[above], row.at[above], self.partner)

    def far(self):
        mail, row = self.mail, self.row
        far = self.place.row_slot(y=2)
        mail.receive(self.up_on, row.at[far, self.first], self.near_down)
        mail.receive(self.down_on, row.at[far, self.second], self.near_up)
        mail.send(self.cross[3], row.at[far], row.at[far], self.partner)

    def end(self):
        for number, y in ((0, 0), (1, -1), (2, 1), (3, 2)):
            landed = self.row.at[self.place.row_slot(y=y, other_core=True)]
            self.mail.receive(self.cross[number], landed, self.partner)
        self.keep.wait()


OTHER = {"x": "z", "z": "x"}


class ColumnRings:
    def __init__(self, place, mail, col):
        self.place, self.mail, self.col, self.numbers = place, mail, col, {}
        first, second, first_cut, second_cut = spans(col.shape[1])
        self.halves = {"x": (first, first_cut), "z": (second, second_cut)}

    def number(self, *key):
        if key not in self.numbers:
            self.numbers[key] = self.mail.number()
        return self.numbers[key]

    def ref(self, axis, along, across, span):
        x, z = (along, across) if axis == "x" else (across, along)
        return self.col.at[self.place.column_slot(x=x, z=z), span]

    def to(self, axis, step):
        return self.place.at(**{axis: step})

    def push(self, axis, step, half, across, span, along=0):
        ref = self.ref(axis, along, across, span)
        self.mail.send(self.number(axis, step, half, across, along), ref, ref, self.to(axis, step))

    def pull(self, axis, step, half, across, span, along=0):
        ref = self.ref(axis, along - step, across, span)
        self.mail.receive(self.number(axis, step, half, across, along), ref, self.to(axis, -step))

    def pass_on(self, axis, half, across):
        span = self.halves[half][0]
        for step in (1, -1):
            self.push(axis, step, half, across, span)
        if half == axis:
            ref = self.ref(axis, 0, across, span)
            self.mail.send(self.number(axis, "far", half, across), ref, ref, self.to(axis, 2))

    def take(self, axis, step, half, across):
        self.pull(axis, step, half, across, self.halves[half][0])
        if half != axis:
            self.push(axis, step, half, across, self.halves[half][1][0 if step == 1 else 1], along=-step)

    def take_far(self, axis, half, across):
        if half == axis:
            ref = self.ref(axis, 2, across, self.halves[half][0])
            self.mail.receive(self.number(axis, "far", half, across), ref, self.to(axis, 2))
        else:
            for step, part in ((1, 0), (-1, 1)):
                self.pull(axis, step, half, across, self.halves[half][1][part], along=-step)

    def start(self):
        for axis in ("x", "z"):
            self.pass_on(axis, axis, 0)
        for axis in ("x", "z"):
            self.pass_on(axis, OTHER[axis], 0)

    def first_ring(self):
        for step in (1, -1):
            for axis in ("x", "z"):
                self.take(axis, step, axis, 0)
                self.pass_on(OTHER[axis], axis, -step)

    def first_ring_far(self):
        for axis in ("x", "z"):
            self.take_far(axis, axis, 0)
            self.pass_on(OTHER[axis], axis, 2)

    def second_ring(self, across):
        for step in (1, -1):
            for axis in ("x", "z"):
                self.take(axis, step, OTHER[axis], across)

    def last(self):
        for across in (0, -1, 1, 2):
            for axis in ("x", "z"):
                self.take_far(axis, OTHER[axis], across)


def enter(place, far):
    barrier = pltpu.get_barrier_semaphore()
    near = [place.at(x=1), place.at(x=-1), place.at(z=1), place.at(z=-1), place.at(y=1), place.at(y=-1)]
    near.append(place.at(other_core=True))
    if far:
        near += [place.at(x=2), place.at(y=2), place.at(z=2)]
    target, source = place.spread_to(), place.spread_from()
    moves = jnp.logical_not(is_here(target, place))
    for device in near:
        pl.semaphore_signal(barrier, inc=1, device_id=device, device_id_type=MESH)

    @pl.when(moves)
    def _():
        for device in (target, source):
            pl.semaphore_signal(barrier, inc=1, device_id=device, device_id_type=MESH)

    pl.semaphore_wait(barrier, len(near) + jnp.where(moves, 2, 0))


HIGH = lax.Precision.HIGH
BF16 = jnp.bfloat16
F32 = jnp.float32
LANES = 128
WIDE = 2 * LANES


def contract(left_side, right_side, left_dim, right_dim, precision=HIGHEST):
    return lax.dot_general(
        left_side,
        right_side,
        (((left_dim,), (right_dim,)), ((), ())),
        precision=precision,
        preferred_element_type=F32,
    )


def split(value):
    high = value.astype(BF16).astype(F32)
    return high, value - high


def left_lanes(shape):
    return lax.broadcasted_iota(jnp.int32, shape, len(shape) - 1) < LANES // 2


def swap_halves(value):
    return pltpu.roll(value, LANES // 2, 1)


def unpack(packed, wide, start):
    rows = packed.shape[0] // 3
    tail = packed[pl.ds(2 * rows, rows), :]
    left = left_lanes(tail.shape)
    wide[pl.ds(start, 2 * rows), 0:LANES] = packed[pl.ds(0, 2 * rows), :]
    wide[pl.ds(start, rows), LANES:WIDE] = jnp.where(left, tail, 0.0)
    wide[pl.ds(start + rows, rows), LANES:WIDE] = jnp.where(left, swap_halves(tail), 0.0)


def unpack_split(packed, parts, start, lane=0):
    rows = packed.shape[0] // 3
    high, low = split(packed[pl.ds(0, 2 * rows), :])
    parts[pl.ds(start, 2 * rows), lane : lane + LANES] = low.astype(BF16)
    parts[pl.ds(start, 2 * rows), lane + LANES : lane + 2 * LANES] = high.astype(BF16)
    high, low = split(packed[pl.ds(2 * rows, rows), :])
    left = left_lanes(high.shape)
    ends = slice(lane + 2 * LANES, lane + 3 * LANES)
    parts[pl.ds(start, rows), ends] = jnp.where(left, high, swap_halves(low)).astype(BF16)
    parts[pl.ds(start + rows, rows), ends] = jnp.where(left, swap_halves(high), low).astype(BF16)


def coefficient_steps(panels, width, total_ref, factor_ref, of_y, of_v, of_w):
    size = panels * width

    def begin():
        rows = lax.broadcasted_iota(jnp.int32, (size, WIDE), 0)
        cols = lax.broadcasted_iota(jnp.int32, (size, WIDE), 1)
        eye = jnp.where(rows == cols, 1.0, 0.0)
        zero = jnp.zeros((size, WIDE), F32)
        for ref, first, at in ((of_y, 0, 2), (of_v, 2 * size, 1)):
            ref[:, 0:LANES] = total_ref[pl.ds(first, size), :]
            ref[:, LANES:WIDE] = total_ref[pl.ds(first + size, size), :]
            ref[:, WIDE * at : WIDE * (at + 1)] = eye
            ref[:, WIDE * (3 - at) : WIDE * (4 - at)] = zero

    def step(panel):
        start = panel * width
        here = slice(start, start + width)
        of_x = of_y[here, :]
        if panel:
            before = slice(0, start)
            of_x = of_x - contract(of_w[before, here], of_v[before, :], 0, 0)
            of_x = of_x - contract(of_v[before, here], of_w[before, :], 0, 0)
        factor = factor_ref[panel]
        scaled = contract(factor, of_x, 0, 0)
        middle = contract(scaled[:, here], factor, 1, 0)
        of_w[here, :] = scaled - 0.5 * contract(middle, of_v[here, :], 1, 0)

    return begin, step


CHUNK = 128


def factors_kernel(
    panels,
    width,
    v_ref,
    matrix,
    factors,
    right,
    left_high,
    left_low,
    w_ref,
    stage,
    high,
    low,
    row_v,
    row_y,
    col_v,
    col_y,
    row_wide,
    flat_v,
    wide_y,
    partial,
    swap,
    sums,
    near,
    share_sum,
    own,
    factor_ref,
    grams_ref,
    total_ref,
    grams_swap,
    grams_sum,
    grams_y,
    grams_x,
    grams_z,
    of_y,
    of_v,
    of_w,
    mixing,
    share_v,
    share_y,
    send_sem,
    recv_sem,
    local_sem,
    stage_sem,
):
    place = Place()
    rows = own.shape[0]
    size = panels * width
    share = v_ref.shape[1]
    chunks = matrix.shape[0] // CHUNK
    partner = place.at(other_core=True)

    def load(chunk):
        return pltpu.make_async_copy(matrix.at[pl.ds(chunk * CHUNK, CHUNK)], stage.at[chunk % 2], stage_sem.at[chunk % 2])

    load(0).start()
    load(1).start()
    factors_here = pltpu.make_async_copy(factors, factor_ref, local_sem.at[3])
    factors_here.start()
    mixing[...] = jnp.zeros_like(mixing)
    mixing[0:size, 0:share] = v_ref[...]
    turned = mixing[:, 0:WIDE].T
    own[0:share, :] = turned[0:share, 0:LANES]
    near_rows, far_rows = turned[0 : share // 2, LANES:], turned[share // 2 : share, LANES:]
    own[share:, :] = jnp.where(left_lanes(near_rows.shape), near_rows, swap_halves(far_rows))
    enter(place, True)
    mail = Mail(send_sem, recv_sem)
    spread_v, spread_y = Spread(place, mail), Spread(place, mail)
    ring_v = RowRing(place, mail, own, row_v, local_sem.at[2])
    ring_y = RowRing(place, mail, share_sum, row_y, local_sem.at[4])
    rings_v, rings_y = ColumnRings(place, mail, col_v), ColumnRings(place, mail, col_y)
    mine = place.column_slot()
    todo = list(range(chunks))

    def convert(count):
        for _ in range(count):
            chunk = todo.pop(0)
            load(chunk).wait()
            top, rest = split(stage[chunk % 2])
            high[pl.ds(chunk * CHUNK, CHUNK), :] = top.astype(BF16)
            low[pl.ds(chunk * CHUNK, CHUNK), :] = rest.astype(BF16)
            if chunk + 2 < chunks:
                load(chunk + 2).start()

    spread_v.start(own, col_v.at[place.spread_slot()], col_v.at[mine], local_sem.at[0])
    ring_v.start()
    convert(3)
    spread_v.arrived()
    rings_v.start()
    ring_v.near()
    convert(2)
    rings_v.first_ring()
    convert(1)
    rings_v.second_ring(0)
    ring_v.far()
    convert(1)
    rings_v.first_ring_far()
    convert(1)
    rings_v.second_ring(-1)
    convert(1)
    rings_v.second_ring(1)
    convert(1)
    rings_v.second_ring(2)
    ring_v.end()
    for slot in range(8):
        unpack(row_v.at[slot], row_wide, slot * share)
    flat_v[...] = row_wide[...].T[0:size, :]
    gram = contract(flat_v[...], row_wide[...], 1, 0, HIGH) * 0.125
    grams_ref[2 * size : 3 * size, :] = gram[:, 0:LANES]
    grams_ref[3 * size : 4 * size, :] = gram[:, LANES:]
    rings_v.last()
    for slot in range(16):
        unpack_split(col_v.at[slot], right, slot * share)

    first, second, _, _ = spans(rows)
    near_up, near_down = place.at(y=1), place.at(y=-1)
    across = {y: mail.number() for y in (2, 1, -1, 0)}
    far_up, far_down, up_now, up_later, down_now, down_later = (mail.number() for _ in range(6))
    left = left_lanes((share // 2, LANES))

    def product(y):
        block = lax.rem(place.y + y + SIDE, SIDE)
        here = pl.ds(pl.multiple_of(block * 2 * share, 2 * share), 2 * share)
        top = jnp.dot(high[here, :], right[:, 0 : 3 * LANES], preferred_element_type=F32)
        rest = jnp.dot(low[here, :], right[:, LANES : 3 * LANES], preferred_element_type=F32)
        main = top[:, 0:LANES] + top[:, LANES : 2 * LANES] + rest[:, 0:LANES]
        tail = top[:, 2 * LANES :] + rest[:, LANES:]
        tail = tail + swap_halves(tail)
        wide_y[here, 0:LANES] = main
        wide_y[here, LANES:WIDE] = jnp.where(left_lanes(tail.shape), tail, 0.0)
        for core in range(2):
            slot = (y % SIDE) * 2 + core
            start = core * share
            partial[slot, 0:share, :] = main[start : start + share]
            upper, lower = tail[start : start + share // 2], tail[start + share // 2 : start + share]
            partial[slot, share:, :] = jnp.where(left, upper, lower)
        slot = (y % SIDE) * 2 + 1 - place.core
        mail.send(across[y], partial.at[slot], swap.at[y % SIDE], partner)

    def add_across(y):
        slot = y % SIDE
        mail.receive(across[y], swap.at[slot], partner)
        sums[slot, :, :] = partial[slot * 2 + place.core] + swap[slot]

    product(2)
    product(1)
    add_across(2)
    mail.send(far_up, sums.at[2, first], near.at[0, first], near_up)
    mail.send(far_down, sums.at[2, second], near.at[0, second], near_down)
    product(-1)
    add_across(1)
    mail.send(up_now, sums.at[1, second], near.at[1, second], near_up)
    product(0)
    add_across(-1)
    mail.send(down_now, sums.at[3, first], near.at[2, first], near_down)
    gram = contract(flat_v[...], wide_y[...], 1, 0, HIGH)
    grams_ref[0:size, :] = gram[:, 0:LANES]
    grams_ref[size : 2 * size, :] = gram[:, LANES:]

    half = grams_ref.shape[0] // 2
    part = half // SIDE
    cores = mail.number()
    mail.send(cores, grams_ref.at[pl.ds(pl.multiple_of((1 - place.core) * half, 8), half)], grams_swap, partner)

    def exchange(axis, source, landing):
        numbers = [mail.number() for _ in range(1, SIDE)]
        for step in range(1, SIDE):
            mail.send(numbers[step - 1], source(step), landing.at[step - 1], place.at(**{axis: step}))

        def arrived():
            for step in range(1, SIDE):
                mail.receive(numbers[step - 1], landing.at[step - 1], place.at(**{axis: -step}))
            return landing[0] + landing[1] + landing[2]

        return arrived

    def quarter(step):
        return pl.ds(pl.multiple_of(lax.rem(place.y + step, SIDE) * part, 8), part)

    mail.receive(far_up, near.at[0, first], near_down)
    sums[1, first, :] = sums[1, first, :] + near[0, first, :]
    mail.send(up_later, sums.at[1, first], near.at[1, first], near_up)
    mail.receive(far_down, near.at[0, second], near_up)
    sums[3, second, :] = sums[3, second, :] + near[0, second, :]
    mail.send(down_later, sums.at[3, second], near.at[2, second], near_down)
    add_across(0)
    mail.receive(cores, grams_swap, partner)
    core_half = pl.ds(pl.multiple_of(place.core * half, 8), half)
    grams_sum[pl.ds(0, half), :] = grams_ref[core_half, :] + grams_swap[...]
    over_y = exchange("y", lambda step: grams_sum.at[quarter(step)], grams_y)
    mail.receive(up_now, near.at[1, second], near_down)
    mail.receive(down_now, near.at[2, first], near_up)
    mail.receive(up_later, near.at[1, first], near_down)
    mail.receive(down_later, near.at[2, second], near_up)
    share_sum[...] = sums[0] + near[1] + near[2]

    spread_y.start(share_sum, col_y.at[place.spread_slot()], col_y.at[mine], local_sem.at[1])
    ring_y.start()
    grams_sum[pl.ds(half, part), :] = grams_sum[quarter(0), :] + over_y()
    over_x = exchange("x", lambda step: grams_sum.at[pl.ds(half, part)], grams_x)
    spread_y.arrived()
    rings_y.start()
    grams_sum[pl.ds(half + part, part), :] = grams_sum[pl.ds(half, part), :] + over_x()
    over_z = exchange("z", lambda step: grams_sum.at[pl.ds(half + part, part)], grams_z)

    def total_rows(y, other_core=False):
        core = 1 - place.core if other_core else place.core
        start = core * half + lax.rem(place.y + y + SIDE, SIDE) * part
        return total_ref.at[pl.ds(pl.multiple_of(start, 8), part)]

    back_y = [mail.number() for _ in range(1, SIDE)]
    back_core = [mail.number() for _ in range(SIDE)]
    ring_y.near()
    rings_y.first_ring()
    start = place.core * half + place.y * part
    total_ref[pl.ds(pl.multiple_of(start, 8), part), :] = grams_sum[pl.ds(half + part, part), :] + over_z()
    for step in range(1, SIDE):
        mail.send(back_y[step - 1], total_rows(0), total_rows(0), place.at(y=step))
    mail.send(back_core[0], total_rows(0), total_rows(0), partner)
    rings_y.second_ring(0)
    ring_y.far()
    rings_y.first_ring_far()
    rings_y.second_ring(-1)
    for step in range(1, SIDE):
        mail.receive(back_y[step - 1], total_rows(-step), place.at(y=-step))
        mail.send(back_core[step], total_rows(-step), total_rows(-step), partner)
    rings_y.second_ring(1)
    for step in range(SIDE):
        mail.receive(back_core[step], total_rows(-step, True), partner)
    factors_here.wait()

    begin, step = coefficient_steps(panels, width, total_ref, factor_ref, of_y, of_v, of_w)

    def mix():
        mixing[...] = jnp.zeros_like(mixing)
        of_d, of_c = of_w[:, WIDE : 2 * WIDE], of_w[:, 2 * WIDE :]
        mixing[0:size, 0:WIDE] = of_d
        mixing[:, 0:WIDE] = mixing[:, 0:WIDE] + mixing[:, 0:WIDE].T
        mixing[0:size, WIDE:] = of_c

    def store_left(value, start, lane, low_lane):
        left = left_lanes((share, LANES))
        for at in range(2):
            top, rest = split(value[:, at * LANES : (at + 1) * LANES])
            if at:
                top = jnp.where(left, top, swap_halves(top))
                rest = jnp.where(left, rest, swap_halves(rest))
            here = pl.ds(start, share)
            low_here = slice(low_lane + at * LANES, low_lane + (at + 1) * LANES)
            left_low[here, low_here] = rest.astype(BF16)
            if not at:
                left_high[here, lane : lane + LANES] = top.astype(BF16)
            left_high[here, lane + (at + 1) * LANES : lane + (at + 2) * LANES] = top.astype(BF16)

    def left_rows(slot):
        unpack(row_y.at[slot], share_y, 0)
        here = pl.ds(slot * share, share)
        of_right_v = contract(row_wide[here, :], mixing[:, 0:WIDE], 1, 0, HIGH)
        of_right_v = of_right_v + contract(share_y[...], mixing[:, WIDE:], 1, 1, HIGH)
        of_right_y = contract(row_wide[here, :], mixing[:, WIDE:], 1, 0, HIGH)
        store_left(of_right_v, slot * share, 0, 0)
        store_left(of_right_y, slot * share, 3 * LANES, 2 * LANES)

    begin()
    step(0)
    rings_y.second_ring(2)
    step(1)
    step(2)
    step(3)
    step(4)
    step(5)
    mix()
    unpack(own, share_v, 0)
    unpack(share_sum, share_y, 0)
    w_ref[...] = contract(of_w[:, WIDE : 2 * WIDE], share_v[...], 1, 1, HIGH)
    w_ref[...] = w_ref[...] + contract(of_w[:, 2 * WIDE :], share_y[...], 1, 1, HIGH)
    ring_y.end()
    for slot in range(8):
        left_rows(slot)
    rings_y.last()
    for slot in range(16):
        unpack_split(col_y.at[slot], right, slot * share, 3 * LANES)
    spread_v.finish()
    spread_y.finish()
    mail.finish()


def in_vmem(count):
    return [pl.BlockSpec(memory_space=pltpu.VMEM)] * count


def factors_call(v, matrix, factors):
    size, share = v.shape
    rows, lanes = share + share // 2, LANES
    height, length = matrix.shape
    panels, width, _ = factors.shape
    grams = 4 * size
    part = grams // 8
    return pl.pallas_call(
        functools.partial(factors_kernel, panels, width),
        out_shape=(
            jax.ShapeDtypeStruct((length, 6 * lanes), BF16),
            jax.ShapeDtypeStruct((height, 6 * lanes), BF16),
            jax.ShapeDtypeStruct((height, 4 * lanes), BF16),
            jax.ShapeDtypeStruct((size, share), F32),
        ),
        in_specs=in_vmem(1) + [pl.BlockSpec(memory_space=pl.ANY)] * 2,
        out_specs=in_vmem(4),
        scratch_shapes=[
            pltpu.VMEM((2, CHUNK, length), F32),
            pltpu.VMEM((height, length), BF16),
            pltpu.VMEM((height, length), BF16),
            pltpu.VMEM((8, rows, lanes), F32),
            pltpu.VMEM((8, rows, lanes), F32),
            pltpu.VMEM((16, rows, lanes), F32),
            pltpu.VMEM((16, rows, lanes), F32),
            pltpu.VMEM((height, WIDE), F32),
            pltpu.VMEM((size, height), F32),
            pltpu.VMEM((height, WIDE), F32),
            pltpu.VMEM((8, rows, lanes), F32),
            pltpu.VMEM((SIDE, rows, lanes), F32),
            pltpu.VMEM((SIDE, rows, lanes), F32),
            pltpu.VMEM((3, rows, lanes), F32),
            pltpu.VMEM((rows, lanes), F32),
            pltpu.VMEM((rows, lanes), F32),
            pltpu.VMEM(factors.shape, F32),
            pltpu.VMEM((grams, lanes), F32),
            pltpu.VMEM((grams, lanes), F32),
            pltpu.VMEM((SIDE * part, lanes), F32),
            pltpu.VMEM((6 * part, lanes), F32),
            pltpu.VMEM((3, part, lanes), F32),
            pltpu.VMEM((3, part, lanes), F32),
            pltpu.VMEM((3, part, lanes), F32),
            pltpu.VMEM((size, 3 * WIDE), F32),
            pltpu.VMEM((size, 3 * WIDE), F32),
            pltpu.VMEM((size, 3 * WIDE), F32),
            pltpu.VMEM((WIDE, 2 * WIDE), F32),
            pltpu.VMEM((share, WIDE), F32),
            pltpu.VMEM((share, WIDE), F32),
            pltpu.SemaphoreType.DMA((192,)),
            pltpu.SemaphoreType.DMA((192,)),
            pltpu.SemaphoreType.DMA((5,)),
            pltpu.SemaphoreType.DMA((2,)),
        ],
        compiler_params=pltpu.CompilerParams(collective_id=0, has_side_effects=True, vmem_limit_bytes=42 * 1024 * 1024),
        cost_estimate=pl.CostEstimate(flops=50_000_000_000, bytes_accessed=100_000_000, transcendentals=0),
        name="factors",
    )(v, matrix, factors)


TILE = 256


def update_kernel(matrix_ref, right_ref, high_ref, low_ref, w_in, out_ref, w_out):
    right = right_ref[...]
    change = contract(high_ref[...], right, 1, 1, None)
    low_v, low_y = low_ref[:, 0 : 2 * LANES], low_ref[:, 2 * LANES :]
    change = change + contract(low_v, right[:, LANES : 3 * LANES], 1, 1, None)
    change = change + contract(low_y, right[:, 4 * LANES :], 1, 1, None)
    out_ref[...] = matrix_ref[...] - change
    w_out[...] = w_in[...]


def update_call(matrix, right, left_high, left_low, w):
    height, length = matrix.shape

    def whole(array):
        return pl.BlockSpec(array.shape, lambda tile: (0, 0), pipeline_mode=pl.Buffered(1))

    return pl.pallas_call(
        update_kernel,
        grid=(length // TILE,),
        out_shape=(jax.ShapeDtypeStruct(matrix.shape, F32), jax.ShapeDtypeStruct(w.shape, F32)),
        in_specs=[
            pl.BlockSpec((height, TILE), lambda tile: (0, tile)),
            pl.BlockSpec((TILE, right.shape[1]), lambda tile: (tile, 0)),
            whole(left_high),
            whole(left_low),
            whole(w),
        ],
        out_specs=[pl.BlockSpec((height, TILE), lambda tile: (0, tile)), pl.BlockSpec(w.shape, lambda tile: (0, 0))],
        compiler_params=pltpu.CompilerParams(dimension_semantics=("arbitrary",), vmem_limit_bytes=14 * 1024 * 1024),
        name="update",
    )(matrix, right, left_high, left_low, w)


def per_device(trailing, v_panels, t_panels):
    panels, width, share = v_panels.shape
    size = panels * width
    v = v_panels.reshape(size, share)
    right, left_high, left_low, w = factors_call(v, trailing, t_panels)
    matrix, w = update_call(trailing, right, left_high, left_low, w)
    return (matrix, w.reshape(panels, width, share))


def solution(mesh):
    return jax.shard_map(
        per_device,
        mesh=mesh,
        in_specs=(P("pr", "pc"), P(None, None, ("pr", "pc")), P()),
        out_specs=(P("pr", "pc"), P(None, None, ("pr", "pc"))),
        check_vma=False,
    )
```

time: 355 us -> 95.7 us (0.27)
  waiting for transfers between devices: 190 us -> 0 us
  Pallas kernels: 0 us -> 92.6 us
  matrix products: 74.1 us -> 0 us
  blocking collectives: 36.6 us -> 0 us
  local copies, waits for them, and re-layouts: 24.1 us -> 2.25 us
  between operations: 14 us -> 0.7 us
  starting transfers between devices: 11 us -> 0 us
  other arithmetic: 4.12 us -> 0.01 us
    psum x1 -> x0, waiting for transfers between devices: 118 us -> none  [per_device(): grams = lax.psum(grams, ('pr', 'pc'))]
    pallas_call x0 -> x2, Pallas kernels: none -> 92.6 us  [the longest x1 80 us: factors_call(): pl.pallas_call(functools.partial(factors_kernel, panels, width), out_shap...]
    dot_general x31 -> x0, matrix products: 74.1 us -> none  [contract(): lax.dot_general(left_side, right_side, (((left_dim,), (right_dim,)), ((),...]
    all_gather x2 -> x0, waiting for transfers between devices: 53.5 us -> none  [columns(): lax.all_gather(lax.ppermute(own, ('pr', 'pc'), moves), 'pr', axis=1, tile...]
    all_gather x2 -> x0, blocking collectives: 36.6 us -> none  [the longest x1 20.7 us: per_device(): y_row = lax.all_gather(y_own, 'pc', axis=1, tiled=True)]
    slice x21 -> x0, local copies, waits for them, and re-layouts: 18 us -> none  [the longest x15 14.3 us: small_coefficients(): left = jnp.concatenate([done[:, here], gram_v[before, here]], axis=0)]
    reduce_scatter x1 -> x0, waiting for transfers between devices: 13.6 us -> none  [per_device(): y_own = lax.psum_scatter(partial_y, 'pc', scatter_dimension=1, tiled=True)]
    ppermute x2 -> x0, starting transfers between devices: 10.8 us -> none  [columns(): lax.ppermute(own, ('pr', 'pc'), moves)]
  transfers between devices with their start and end apart: 6 -> 0, of which waited for: 4 -> 0; matrix products, arithmetic and copies ran while one was open for 18% -> 0% of each run, Pallas kernels for 0% -> 0%
where the time goes in v4:
time: 95.7 us; the launch traced here: 95.5 us
  Pallas kernels  92.6 us (97%)
  local copies, waits for them, and re-layouts  2.25 us (2%)
    pallas_call x1, Pallas kernels, factors_call(): pl.pallas_call(functools.partial(factors_kernel, panels, width), out_shap...  80 us
    pallas_call x1, Pallas kernels, update_call(): pl.pallas_call(update_kernel, grid=(length // TILE,), out_shape=(jax.Shap...  12.6 us
    unnamed x12, local copies, waits for them, and re-layouts  2.25 us

profile of v4, /device:TPU:1, one launch (start us, length us, event | category | flops | bytes accessed | tf_op | source)
XLA Modules:
  0.0 95.5 jit_solution(1644167852412286033)
XLA Ops:
  0.6 0.0 slice-start
  0.6 0.0 copy-start
  0.7 1.1 %copy-done = f32[6,32,160]{2,1,0:T(8,128)S(1)} copy-done((f32[6,32,160]{2,1,0:T(8,128)S(1)}, f32[6,32,160]{2,1,0:T(8,128)}, u32[]{:S(2)}) %copy-start) | copy-done | bytes 122904
  1.7 0.0 copy-start.1
  1.7 1.2 %copy-done.1 = f32[6,32,32]{2,1,0:T(8,128)S(1)} copy-done((f32[6,32,32]{2,1,0:T(8,128)S(1)}, f32[6,32,32]{2,1,0:T(8,128)}, u32[]{:S(2)}) %copy-start.1) | copy-done | bytes 24600
  2.9 0.0 slice-start.1
  2.9 0.0 slice-start.2
  2.9 0.0 slice-start.3
  2.9 80.0 %factors.2 = (bf16[2560,768]{1,0:T(8,128)(2,1)S(1)}, bf16[1280,768]{1,0:T(8,128)(2,1)S(1)}, bf16[1280,512]{1,0:T(8,128)(2,1)S(1)}, f32[192,160]{1,0:T(8,128)S(1)}) custom-call(f32[192,160]{1,0:T(8,128)S(1)} %bitcast.4, f32[1280,2560]{1,0:T(8,128)} %matrix_ref.1, f32[6,32,32]{2,1,0:T(8,128)S(1)} %copy-done.1), custom_call_target="tpu_custom_call" | custom-call | flops 49999998976 | bytes 100000000 | tf_op jit(solution)/shard_map/factors/pallas_call | solution.py:661
  82.8 0.0 slice-done
  82.9 0.0 slice-done.1
  82.9 0.0 slice-done.2
  82.9 0.0 slice-done.3
  82.9 12.6 %update.1 = (f32[1280,2560]{1,0:T(8,128)}, f32[192,160]{1,0:T(8,128)}) custom-call(f32[1280,2560]{1,0:T(8,128)S(1)} %bitcast.3, bf16[2560,768]{1,0:T(8,128)(2,1)S(1)} %get-tuple-element.8.right_ref, bf16[1280,768]{1,0:T(8,128)(2,1)S(1)} %get-tuple-element.9.high_ref, bf16[1280,512]{1,0:T(8,128)(2,1)S(1)} %get-tuple-element.10.low_ref, ...), custom_call_target="tpu_custom_call" | custom-call | tf_op jit(solution)/shard_map/update/pallas_call | solution.py:732
  (1 shorter events, 0.0 us)
Async XLA Ops:
  0.6 82.2 %slice-start = ((s8[13107200]{0:T(1024)(128)(4,1)}), s8[4194304]{0:T(1024)(128)(4,1)S(1)}, s32[]{:S(2)}) async-start(s8[13107200]{0:T(1024)(128)(4,1)} %bitcast.2), calls=%async_computation | async-start | bytes 8388608
  0.6 1.1 %copy-start = (f32[6,32,160]{2,1,0:T(8,128)S(1)}, f32[6,32,160]{2,1,0:T(8,128)}, u32[]{:S(2)}) copy-start(f32[6,32,160]{2,1,0:T(8,128)} %param.4) | copy-start | bytes 368644
  1.7 1.2 %copy-start.1 = (f32[6,32,32]{2,1,0:T(8,128)S(1)}, f32[6,32,32]{2,1,0:T(8,128)}, u32[]{:S(2)}) copy-start(f32[6,32,32]{2,1,0:T(8,128)} %factors.3) | copy-start | bytes 73732
  2.9 80.0 %slice-start.1 = ((s8[13107200]{0:T(1024)(128)(4,1)}), s8[4194304]{0:T(1024)(128)(4,1)S(1)}, s32[]{:S(2)}) async-start(s8[13107200]{0:T(1024)(128)(4,1)} %bitcast.2), calls=%async_computation.1 | async-start | bytes 8388608
  2.9 80.0 %slice-start.2 = ((s8[13107200]{0:T(1024)(128)(4,1)}), s8[4194304]{0:T(1024)(128)(4,1)S(1)}, s32[]{:S(2)}) async-start(s8[13107200]{0:T(1024)(128)(4,1)} %bitcast.2), calls=%async_computation.2 | async-start | bytes 8388608
  2.9 80.0 %slice-start.3 = ((s8[13107200]{0:T(1024)(128)(4,1)}), s8[524288]{0:T(1024)(128)(4,1)S(1)}, s32[]{:S(2)}) async-start(s8[13107200]{0:T(1024)(128)(4,1)} %bitcast.2), calls=%async_computation.3 | async-start | bytes 1048576

commit v5 on v4

--- a/solution.py
+++ b/solution.py
@@ -257,7 +257,7 @@
                 self.take_far(axis, OTHER[axis], across)
 
 
-def enter(place, far):
+def greet(place, far):
     barrier = pltpu.get_barrier_semaphore()
     near = [place.at(x=1), place.at(x=-1), place.at(z=1), place.at(z=-1), place.at(y=1), place.at(y=-1)]
     near.append(place.at(other_core=True))
@@ -273,7 +273,7 @@
         for device in (target, source):
             pl.semaphore_signal(barrier, inc=1, device_id=device, device_id_type=MESH)
 
-    pl.semaphore_wait(barrier, len(near) + jnp.where(moves, 2, 0))
+    return len(near) + jnp.where(moves, 2, 0)
 
 
 HIGH = lax.Precision.HIGH
@@ -358,6 +358,8 @@
 
 
 CHUNK = 128
+NEAR = [(x, z) for x in (0, 1, -1) for z in (0, 1, -1)]
+FAR = [(x, z) for x in (0, 1, -1, 2) for z in (0, 1, -1, 2) if 2 in (x, z)]
 
 
 def factors_kernel(
@@ -386,6 +388,7 @@
     near,
     share_sum,
     own,
+    v_own,
     factor_ref,
     grams_ref,
     total_ref,
@@ -415,17 +418,21 @@
     def load(chunk):
         return pltpu.make_async_copy(matrix.at[pl.ds(chunk * CHUNK, CHUNK)], stage.at[chunk % 2], stage_sem.at[chunk % 2])
 
+    v_here = pltpu.make_async_copy(v_ref, v_own, local_sem.at[0])
+    v_here.start()
+    factors_here = pltpu.make_async_copy(factors, factor_ref, local_sem.at[3])
+    factors_here.start()
     load(0).start()
     load(1).start()
-    factors_here = pltpu.make_async_copy(factors, factor_ref, local_sem.at[3])
-    factors_here.start()
+    greeted = greet(place, True)
     mixing[...] = jnp.zeros_like(mixing)
-    mixing[0:size, 0:share] = v_ref[...]
+    v_here.wait()
+    mixing[0:size, 0:share] = v_own[...]
     turned = mixing[:, 0:WIDE].T
     own[0:share, :] = turned[0:share, 0:LANES]
     near_rows, far_rows = turned[0 : share // 2, LANES:], turned[share // 2 : share, LANES:]
     own[share:, :] = jnp.where(left_lanes(near_rows.shape), near_rows, swap_halves(far_rows))
-    enter(place, True)
+    pl.semaphore_wait(pltpu.get_barrier_semaphore(), greeted)
     mail = Mail(send_sem, recv_sem)
     spread_v, spread_y = Spread(place, mail), Spread(place, mail)
     ring_v = RowRing(place, mail, own, row_v, local_sem.at[2])
@@ -444,24 +451,28 @@
             if chunk + 2 < chunks:
                 load(chunk + 2).start()
 
+    def unpack_columns(col, lane, chips):
+        for x, z in chips:
+            slot = place.column_slot(x=x, z=z)
+            unpack_split(col.at[slot], right, pl.multiple_of(slot * share, 32), lane)
+
     spread_v.start(own, col_v.at[place.spread_slot()], col_v.at[mine], local_sem.at[0])
-    ring_v.start()
-    convert(3)
+    convert(4)
     spread_v.arrived()
     rings_v.start()
-    ring_v.near()
+    ring_v.start()
     convert(2)
     rings_v.first_ring()
+    ring_v.near()
     convert(1)
     rings_v.second_ring(0)
-    ring_v.far()
     convert(1)
     rings_v.first_ring_far()
+    ring_v.far()
     convert(1)
     rings_v.second_ring(-1)
     convert(1)
     rings_v.second_ring(1)
-    convert(1)
     rings_v.second_ring(2)
     ring_v.end()
     for slot in range(8):
@@ -470,9 +481,9 @@
     gram = contract(flat_v[...], row_wide[...], 1, 0, HIGH) * 0.125
     grams_ref[2 * size : 3 * size, :] = gram[:, 0:LANES]
     grams_ref[3 * size : 4 * size, :] = gram[:, LANES:]
+    unpack_columns(col_v, 0, NEAR)
     rings_v.last()
-    for slot in range(16):
-        unpack_split(col_v.at[slot], right, slot * share)
+    unpack_columns(col_v, 0, FAR)
 
     first, second, _, _ = spans(rows)
     near_up, near_down = place.at(y=1), place.at(y=-1)
@@ -557,11 +568,11 @@
     share_sum[...] = sums[0] + near[1] + near[2]
 
     spread_y.start(share_sum, col_y.at[place.spread_slot()], col_y.at[mine], local_sem.at[1])
-    ring_y.start()
     grams_sum[pl.ds(half, part), :] = grams_sum[quarter(0), :] + over_y()
     over_x = exchange("x", lambda step: grams_sum.at[pl.ds(half, part)], grams_x)
     spread_y.arrived()
     rings_y.start()
+    ring_y.start()
     grams_sum[pl.ds(half + part, part), :] = grams_sum[pl.ds(half, part), :] + over_x()
     over_z = exchange("z", lambda step: grams_sum.at[pl.ds(half + part, part)], grams_z)
 
@@ -572,16 +583,16 @@
 
     back_y = [mail.number() for _ in range(1, SIDE)]
     back_core = [mail.number() for _ in range(SIDE)]
+    rings_y.first_ring()
     ring_y.near()
-    rings_y.first_ring()
     start = place.core * half + place.y * part
     total_ref[pl.ds(pl.multiple_of(start, 8), part), :] = grams_sum[pl.ds(half + part, part), :] + over_z()
     for step in range(1, SIDE):
         mail.send(back_y[step - 1], total_rows(0), total_rows(0), place.at(y=step))
     mail.send(back_core[0], total_rows(0), total_rows(0), partner)
     rings_y.second_ring(0)
+    rings_y.first_ring_far()
     ring_y.far()
-    rings_y.first_ring_far()
     rings_y.second_ring(-1)
     for step in range(1, SIDE):
         mail.receive(back_y[step - 1], total_rows(-step), place.at(y=-step))
@@ -639,9 +650,9 @@
     ring_y.end()
     for slot in range(8):
         left_rows(slot)
+    unpack_columns(col_y, 3 * LANES, NEAR)
     rings_y.last()
-    for slot in range(16):
-        unpack_split(col_y.at[slot], right, slot * share, 3 * LANES)
+    unpack_columns(col_y, 3 * LANES, FAR)
     spread_v.finish()
     spread_y.finish()
     mail.finish()
@@ -666,7 +677,7 @@
             jax.ShapeDtypeStruct((height, 4 * lanes), BF16),
             jax.ShapeDtypeStruct((size, share), F32),
         ),
-        in_specs=in_vmem(1) + [pl.BlockSpec(memory_space=pl.ANY)] * 2,
+        in_specs=[pl.BlockSpec(memory_space=pltpu.HBM)] * 3,
         out_specs=in_vmem(4),
         scratch_shapes=[
             pltpu.VMEM((2, CHUNK, length), F32),
@@ -685,6 +696,7 @@
             pltpu.VMEM((3, rows, lanes), F32),
             pltpu.VMEM((rows, lanes), F32),
             pltpu.VMEM((rows, lanes), F32),
+            pltpu.VMEM((size, share), F32),
             pltpu.VMEM(factors.shape, F32),
             pltpu.VMEM((grams, lanes), F32),
             pltpu.VMEM((grams, lanes), F32),
@@ -704,13 +716,13 @@
             pltpu.SemaphoreType.DMA((5,)),
             pltpu.SemaphoreType.DMA((2,)),
         ],
-        compiler_params=pltpu.CompilerParams(collective_id=0, has_side_effects=True, vmem_limit_bytes=42 * 1024 * 1024),
+        compiler_params=pltpu.CompilerParams(collective_id=0, has_side_effects=True, vmem_limit_bytes=35 * 1024 * 1024),
         cost_estimate=pl.CostEstimate(flops=50_000_000_000, bytes_accessed=100_000_000, transcendentals=0),
         name="factors",
     )(v, matrix, factors)
 
 
-TILE = 256
+TILE = 512
 
 
 def update_kernel(matrix_ref, right_ref, high_ref, low_ref, w_in, out_ref, w_out):
@@ -726,9 +738,6 @@
 def update_call(matrix, right, left_high, left_low, w):
     height, length = matrix.shape
 
-    def whole(array):
-        return pl.BlockSpec(array.shape, lambda tile: (0, 0), pipeline_mode=pl.Buffered(1))
-
     return pl.pallas_call(
         update_kernel,
         grid=(length // TILE,),
@@ -736,12 +745,10 @@
         in_specs=[
             pl.BlockSpec((height, TILE), lambda tile: (0, tile)),
             pl.BlockSpec((TILE, right.shape[1]), lambda tile: (tile, 0)),
-            whole(left_high),
-            whole(left_low),
-            whole(w),
+            *in_vmem(3),
         ],
         out_specs=[pl.BlockSpec((height, TILE), lambda tile: (0, tile)), pl.BlockSpec(w.shape, lambda tile: (0, 0))],
-        compiler_params=pltpu.CompilerParams(dimension_semantics=("arbitrary",), vmem_limit_bytes=14 * 1024 * 1024),
+        compiler_params=pltpu.CompilerParams(dimension_semantics=("arbitrary",), vmem_limit_bytes=22 * 1024 * 1024),
         name="update",
     )(matrix, right, left_high, left_low, w)
 

time: 95.7 us -> 95.4 us (level)
  no operation moved by 1% of the time
where the time goes in v5:
time: 95.4 us; the launch traced here: 95.2 us
  Pallas kernels  92.2 us (97%)
  local copies, waits for them, and re-layouts  2.25 us (2%)
    pallas_call x1, Pallas kernels, factors_call(): pl.pallas_call(functools.partial(factors_kernel, panels, width), out_shap...  80.3 us
    pallas_call x1, Pallas kernels, update_call(): pl.pallas_call(update_kernel, grid=(length // TILE,), out_shape=(jax.Shap...  12 us
    unnamed x12, local copies, waits for them, and re-layouts  2.25 us

profile of v5, /device:TPU:1, one launch (start us, length us, event | category | flops | bytes accessed | tf_op | source)
XLA Modules:
  0.0 95.2 jit_solution(14512081258836368749)
XLA Ops:
  0.6 0.0 slice-start
  0.6 0.0 copy-start
  0.7 1.1 %copy-done = f32[6,32,160]{2,1,0:T(8,128)S(1)} copy-done((f32[6,32,160]{2,1,0:T(8,128)S(1)}, f32[6,32,160]{2,1,0:T(8,128)}, u32[]{:S(2)}) %copy-start) | copy-done | bytes 122904
  1.7 0.0 copy-start.1
  1.7 1.2 %copy-done.1 = f32[6,32,32]{2,1,0:T(8,128)S(1)} copy-done((f32[6,32,32]{2,1,0:T(8,128)S(1)}, f32[6,32,32]{2,1,0:T(8,128)}, u32[]{:S(2)}) %copy-start.1) | copy-done | bytes 24600
  2.9 0.0 slice-start.1
  2.9 0.0 slice-start.2
  2.9 0.0 slice-start.3
  2.9 80.3 %factors.2 = (bf16[2560,768]{1,0:T(8,128)(2,1)S(1)}, bf16[1280,768]{1,0:T(8,128)(2,1)S(1)}, bf16[1280,512]{1,0:T(8,128)(2,1)S(1)}, f32[192,160]{1,0:T(8,128)S(1)}) custom-call(f32[192,160]{1,0:T(8,128)S(1)} %bitcast.4, f32[1280,2560]{1,0:T(8,128)} %matrix_ref.1, f32[6,32,32]{2,1,0:T(8,128)S(1)} %copy-done.1), custom_call_target="tpu_custom_call" | custom-call | flops 49999998976 | bytes 100000000 | tf_op jit(solution)/shard_map/factors/pallas_call | solution.py:672
  83.2 0.0 slice-done
  83.2 0.0 slice-done.1
  83.2 0.0 slice-done.2
  83.2 0.0 slice-done.3
  83.2 12.0 %update.1 = (f32[1280,2560]{1,0:T(8,128)}, f32[192,160]{1,0:T(8,128)}) custom-call(f32[1280,2560]{1,0:T(8,128)S(1)} %bitcast.3, bf16[2560,768]{1,0:T(8,128)(2,1)S(1)} %get-tuple-element.8.right_ref, bf16[1280,768]{1,0:T(8,128)(2,1)S(1)} %get-tuple-element.9.high_ref, bf16[1280,512]{1,0:T(8,128)(2,1)S(1)} %get-tuple-element.10.low_ref, ...), custom_call_target="tpu_custom_call" | custom-call | tf_op jit(solution)/shard_map/update/pallas_call | solution.py:741
  (1 shorter events, 0.0 us)
Async XLA Ops:
  0.6 82.5 %slice-start = ((s8[13107200]{0:T(1024)(128)(4,1)}), s8[4194304]{0:T(1024)(128)(4,1)S(1)}, s32[]{:S(2)}) async-start(s8[13107200]{0:T(1024)(128)(4,1)} %bitcast.2), calls=%async_computation | async-start | bytes 8388608
  0.6 1.1 %copy-start = (f32[6,32,160]{2,1,0:T(8,128)S(1)}, f32[6,32,160]{2,1,0:T(8,128)}, u32[]{:S(2)}) copy-start(f32[6,32,160]{2,1,0:T(8,128)} %param.4) | copy-start | bytes 368644
  1.7 1.2 %copy-start.1 = (f32[6,32,32]{2,1,0:T(8,128)S(1)}, f32[6,32,32]{2,1,0:T(8,128)}, u32[]{:S(2)}) copy-start(f32[6,32,32]{2,1,0:T(8,128)} %factors.3) | copy-start | bytes 73732
  2.9 80.3 %slice-start.1 = ((s8[13107200]{0:T(1024)(128)(4,1)}), s8[4194304]{0:T(1024)(128)(4,1)S(1)}, s32[]{:S(2)}) async-start(s8[13107200]{0:T(1024)(128)(4,1)} %bitcast.2), calls=%async_computation.1 | async-start | bytes 8388608
  2.9 80.3 %slice-start.2 = ((s8[13107200]{0:T(1024)(128)(4,1)}), s8[4194304]{0:T(1024)(128)(4,1)S(1)}, s32[]{:S(2)}) async-start(s8[13107200]{0:T(1024)(128)(4,1)} %bitcast.2), calls=%async_computation.2 | async-start | bytes 8388608
  2.9 80.3 %slice-start.3 = ((s8[13107200]{0:T(1024)(128)(4,1)}), s8[524288]{0:T(1024)(128)(4,1)S(1)}, s32[]{:S(2)}) async-start(s8[13107200]{0:T(1024)(128)(4,1)} %bitcast.2), calls=%async_computation.3 | async-start | bytes 1048576

commit v6 on v5

--- a/solution.py
+++ b/solution.py
@@ -349,7 +349,7 @@
             before = slice(0, start)
             of_x = of_x - contract(of_w[before, here], of_v[before, :], 0, 0)
             of_x = of_x - contract(of_v[before, here], of_w[before, :], 0, 0)
-        factor = factor_ref[panel]
+        factor = factor_ref[here, factor_ref.shape[1] - width :]
         scaled = contract(factor, of_x, 0, 0)
         middle = contract(scaled[:, here], factor, 1, 0)
         of_w[here, :] = scaled - 0.5 * contract(middle, of_v[here, :], 1, 0)
@@ -367,7 +367,6 @@
     width,
     v_ref,
     matrix,
-    factors,
     right,
     left_high,
     left_low,
@@ -389,7 +388,6 @@
     share_sum,
     own,
     v_own,
-    factor_ref,
     grams_ref,
     total_ref,
     grams_swap,
@@ -411,7 +409,7 @@
     place = Place()
     rows = own.shape[0]
     size = panels * width
-    share = v_ref.shape[1]
+    share = v_ref.shape[1] - width
     chunks = matrix.shape[0] // CHUNK
     partner = place.at(other_core=True)
 
@@ -420,14 +418,12 @@
 
     v_here = pltpu.make_async_copy(v_ref, v_own, local_sem.at[0])
     v_here.start()
-    factors_here = pltpu.make_async_copy(factors, factor_ref, local_sem.at[3])
-    factors_here.start()
     load(0).start()
     load(1).start()
     greeted = greet(place, True)
     mixing[...] = jnp.zeros_like(mixing)
     v_here.wait()
-    mixing[0:size, 0:share] = v_own[...]
+    mixing[0:size, 0:share] = v_own[:, 0:share]
     turned = mixing[:, 0:WIDE].T
     own[0:share, :] = turned[0:share, 0:LANES]
     near_rows, far_rows = turned[0 : share // 2, LANES:], turned[share // 2 : share, LANES:]
@@ -600,9 +596,8 @@
     rings_y.second_ring(1)
     for step in range(SIDE):
         mail.receive(back_core[step], total_rows(-step, True), partner)
-    factors_here.wait()
-
-    begin, step = coefficient_steps(panels, width, total_ref, factor_ref, of_y, of_v, of_w)
+
+    begin, step = coefficient_steps(panels, width, total_ref, v_own, of_y, of_v, of_w)
 
     def mix():
         mixing[...] = jnp.zeros_like(mixing)
@@ -662,11 +657,10 @@
     return [pl.BlockSpec(memory_space=pltpu.VMEM)] * count
 
 
-def factors_call(v, matrix, factors):
-    size, share = v.shape
+def factors_call(v, matrix, panels, width):
+    size, share = v.shape[0], v.shape[1] - width
     rows, lanes = share + share // 2, LANES
     height, length = matrix.shape
-    panels, width, _ = factors.shape
     grams = 4 * size
     part = grams // 8
     return pl.pallas_call(
@@ -677,7 +671,7 @@
             jax.ShapeDtypeStruct((height, 4 * lanes), BF16),
             jax.ShapeDtypeStruct((size, share), F32),
         ),
-        in_specs=[pl.BlockSpec(memory_space=pltpu.HBM)] * 3,
+        in_specs=[pl.BlockSpec(memory_space=pltpu.HBM)] * 2,
         out_specs=in_vmem(4),
         scratch_shapes=[
             pltpu.VMEM((2, CHUNK, length), F32),
@@ -696,8 +690,7 @@
             pltpu.VMEM((3, rows, lanes), F32),
             pltpu.VMEM((rows, lanes), F32),
             pltpu.VMEM((rows, lanes), F32),
-            pltpu.VMEM((size, share), F32),
-            pltpu.VMEM(factors.shape, F32),
+            pltpu.VMEM(v.shape, F32),
             pltpu.VMEM((grams, lanes), F32),
             pltpu.VMEM((grams, lanes), F32),
             pltpu.VMEM((SIDE * part, lanes), F32),
@@ -719,7 +712,7 @@
         compiler_params=pltpu.CompilerParams(collective_id=0, has_side_effects=True, vmem_limit_bytes=35 * 1024 * 1024),
         cost_estimate=pl.CostEstimate(flops=50_000_000_000, bytes_accessed=100_000_000, transcendentals=0),
         name="factors",
-    )(v, matrix, factors)
+    )(v, matrix)
 
 
 TILE = 512
@@ -756,8 +749,8 @@
 def per_device(trailing, v_panels, t_panels):
     panels, width, share = v_panels.shape
     size = panels * width
-    v = v_panels.reshape(size, share)
-    right, left_high, left_low, w = factors_call(v, trailing, t_panels)
+    v = jnp.concatenate([v_panels, t_panels], axis=2).reshape(size, share + width)
+    right, left_high, left_low, w = factors_call(v, trailing, panels, width)
     matrix, w = update_call(trailing, right, left_high, left_low, w)
     return (matrix, w.reshape(panels, width, share))
 

time: 95.4 us -> 94.2 us (0.987)
  local copies, waits for them, and re-layouts: 2.25 us -> 0.02 us
  other arithmetic: 0.01 us -> 1.07 us
    unnamed x12 -> x8, local copies, waits for them, and re-layouts: 2.25 us -> 0.02 us
    concatenate x0 -> x1, other arithmetic: none -> 1.07 us  [per_device(): jnp.concatenate([v_panels, t_panels], axis=2).reshape(size, share + width)]
where the time goes in v6:
time: 94.2 us; the launch traced here: 94.1 us
  Pallas kernels  92.3 us (98%)
  other arithmetic  1.07 us (1%)
    pallas_call x1, Pallas kernels, factors_call(): pl.pallas_call(functools.partial(factors_kernel, panels, width), out_shap...  80.3 us
    pallas_call x1, Pallas kernels, update_call(): pl.pallas_call(update_kernel, grid=(length // TILE,), out_shape=(jax.Shap...  11.9 us

profile of v6, /device:TPU:1, one launch (start us, length us, event | category | flops | bytes accessed | tf_op | source)
XLA Modules:
  0.0 94.1 jit_solution(11357449491526430345)
XLA Ops:
  0.6 1.1 %pad_maximum_fusion = f32[6,32,192]{2,1,0:T(8,128)S(1)} fusion(f32[6,32,32]{2,1,0:T(8,128)} %param.5, f32[6,32,160]{2,1,0:T(8,128)} %param.4), kind=kLoop, calls=%fused_computation | loop fusion | flops 36864 | bytes 294912 | tf_op jit(solution)/shard_map/concatenate | solution.py:752
  1.7 0.0 slice-start
  1.7 0.0 slice-start.1
  1.7 0.0 slice-start.2
  1.7 0.0 slice-start.3
  1.7 80.3 %factors.1 = (bf16[2560,768]{1,0:T(8,128)(2,1)S(1)}, bf16[1280,768]{1,0:T(8,128)(2,1)S(1)}, bf16[1280,512]{1,0:T(8,128)(2,1)S(1)}, f32[192,160]{1,0:T(8,128)S(1)}) custom-call(f32[192,192]{1,0:T(8,128)S(1)} %bitcast.4, f32[1280,2560]{1,0:T(8,128)} %matrix_ref.1), custom_call_target="tpu_custom_call" | custom-call | flops 49999998976 | bytes 100000000 | tf_op jit(solution)/shard_map/factors/pallas_call | solution.py:666
  82.1 0.0 slice-done
  82.1 0.0 slice-done.1
  82.1 0.0 slice-done.2
  82.1 0.0 slice-done.3
  82.1 11.9 %update.1 = (f32[1280,2560]{1,0:T(8,128)}, f32[192,160]{1,0:T(8,128)}) custom-call(f32[1280,2560]{1,0:T(8,128)S(1)} %bitcast.3, bf16[2560,768]{1,0:T(8,128)(2,1)S(1)} %get-tuple-element.8.right_ref, bf16[1280,768]{1,0:T(8,128)(2,1)S(1)} %get-tuple-element.9.high_ref, bf16[1280,512]{1,0:T(8,128)(2,1)S(1)} %get-tuple-element.10.low_ref, ...), custom_call_target="tpu_custom_call" | custom-call | tf_op jit(solution)/shard_map/update/pallas_call | solution.py:734
  (1 shorter events, 0.0 us)
Async XLA Ops:
  1.7 80.4 %slice-start = ((s8[13107200]{0:T(1024)(128)(4,1)}), s8[4194304]{0:T(1024)(128)(4,1)S(1)}, s32[]{:S(2)}) async-start(s8[13107200]{0:T(1024)(128)(4,1)} %bitcast.2), calls=%async_computation | async-start | bytes 8388608
  1.7 80.4 %slice-start.1 = ((s8[13107200]{0:T(1024)(128)(4,1)}), s8[4194304]{0:T(1024)(128)(4,1)S(1)}, s32[]{:S(2)}) async-start(s8[13107200]{0:T(1024)(128)(4,1)} %bitcast.2), calls=%async_computation.1 | async-start | bytes 8388608
  1.7 80.4 %slice-start.2 = ((s8[13107200]{0:T(1024)(128)(4,1)}), s8[4194304]{0:T(1024)(128)(4,1)S(1)}, s32[]{:S(2)}) async-start(s8[13107200]{0:T(1024)(128)(4,1)} %bitcast.2), calls=%async_computation.2 | async-start | bytes 8388608
  1.7 80.4 %slice-start.3 = ((s8[13107200]{0:T(1024)(128)(4,1)}), s8[524288]{0:T(1024)(128)(4,1)S(1)}, s32[]{:S(2)}) async-start(s8[13107200]{0:T(1024)(128)(4,1)} %bitcast.2), calls=%async_computation.3 | async-start | bytes 1048576

commit v7 on v6

--- a/solution.py
+++ b/solution.py
@@ -594,6 +594,7 @@
         mail.receive(back_y[step - 1], total_rows(-step), place.at(y=-step))
         mail.send(back_core[step], total_rows(-step), total_rows(-step), partner)
     rings_y.second_ring(1)
+    rings_y.second_ring(2)
     for step in range(SIDE):
         mail.receive(back_core[step], total_rows(-step, True), partner)
 
@@ -631,7 +632,6 @@
 
     begin()
     step(0)
-    rings_y.second_ring(2)
     step(1)
     step(2)
     step(3)

time: 94.2 us -> 94.2 us (level)
  no operation moved by 1% of the time
where the time goes in v7:
time: 94.2 us; the launch traced here: 94 us
  Pallas kernels  92.2 us (98%)
  other arithmetic  1.07 us (1%)
    pallas_call x1, Pallas kernels, factors_call(): pl.pallas_call(functools.partial(factors_kernel, panels, width), out_shap...  80.3 us
    pallas_call x1, Pallas kernels, update_call(): pl.pallas_call(update_kernel, grid=(length // TILE,), out_shape=(jax.Shap...  11.9 us

profile of v7, /device:TPU:1, one launch (start us, length us, event | category | flops | bytes accessed | tf_op | source)
XLA Modules:
  0.0 94.0 jit_solution(3835626256044828609)
XLA Ops:
  0.6 1.1 %pad_maximum_fusion = f32[6,32,192]{2,1,0:T(8,128)S(1)} fusion(f32[6,32,32]{2,1,0:T(8,128)} %param.5, f32[6,32,160]{2,1,0:T(8,128)} %param.4), kind=kLoop, calls=%fused_computation | loop fusion | flops 36864 | bytes 294912 | tf_op jit(solution)/shard_map/concatenate | solution.py:752
  1.7 0.0 slice-start
  1.7 0.0 slice-start.1
  1.7 0.0 slice-start.2
  1.7 0.0 slice-start.3
  1.7 80.3 %factors.1 = (bf16[2560,768]{1,0:T(8,128)(2,1)S(1)}, bf16[1280,768]{1,0:T(8,128)(2,1)S(1)}, bf16[1280,512]{1,0:T(8,128)(2,1)S(1)}, f32[192,160]{1,0:T(8,128)S(1)}) custom-call(f32[192,192]{1,0:T(8,128)S(1)} %bitcast.4, f32[1280,2560]{1,0:T(8,128)} %matrix_ref.1), custom_call_target="tpu_custom_call" | custom-call | flops 49999998976 | bytes 100000000 | tf_op jit(solution)/shard_map/factors/pallas_call | solution.py:666
  82.0 0.0 slice-done
  82.0 0.0 slice-done.1
  82.1 0.0 slice-done.2
  82.1 0.0 slice-done.3
  82.1 11.9 %update.1 = (f32[1280,2560]{1,0:T(8,128)}, f32[192,160]{1,0:T(8,128)}) custom-call(f32[1280,2560]{1,0:T(8,128)S(1)} %bitcast.3, bf16[2560,768]{1,0:T(8,128)(2,1)S(1)} %get-tuple-element.8.right_ref, bf16[1280,768]{1,0:T(8,128)(2,1)S(1)} %get-tuple-element.9.high_ref, bf16[1280,512]{1,0:T(8,128)(2,1)S(1)} %get-tuple-element.10.low_ref, ...), custom_call_target="tpu_custom_call" | custom-call | tf_op jit(solution)/shard_map/update/pallas_call | solution.py:734
  (1 shorter events, 0.0 us)
Async XLA Ops:
  1.7 80.3 %slice-start = ((s8[13107200]{0:T(1024)(128)(4,1)}), s8[4194304]{0:T(1024)(128)(4,1)S(1)}, s32[]{:S(2)}) async-start(s8[13107200]{0:T(1024)(128)(4,1)} %bitcast.2), calls=%async_computation | async-start | bytes 8388608
  1.7 80.3 %slice-start.1 = ((s8[13107200]{0:T(1024)(128)(4,1)}), s8[4194304]{0:T(1024)(128)(4,1)S(1)}, s32[]{:S(2)}) async-start(s8[13107200]{0:T(1024)(128)(4,1)} %bitcast.2), calls=%async_computation.1 | async-start | bytes 8388608
  1.7 80.3 %slice-start.2 = ((s8[13107200]{0:T(1024)(128)(4,1)}), s8[4194304]{0:T(1024)(128)(4,1)S(1)}, s32[]{:S(2)}) async-start(s8[13107200]{0:T(1024)(128)(4,1)} %bitcast.2), calls=%async_computation.2 | async-start | bytes 8388608
  1.7 80.3 %slice-start.3 = ((s8[13107200]{0:T(1024)(128)(4,1)}), s8[524288]{0:T(1024)(128)(4,1)S(1)}, s32[]{:S(2)}) async-start(s8[13107200]{0:T(1024)(128)(4,1)} %bitcast.2), calls=%async_computation.3 | async-start | bytes 1048576
